TPU v7x, 512 devices: a whole 4x4x16 slice. The times are simulated.
512 devices in a mesh: row: 32 (over z, core), col: 16 (over y, x).
Axes of the slice: x: 4, y: 4, z: 16, core: 2. Of those that a mesh axis runs over, the one named last changes fastest.
Arguments:
- context: bfloat16 [128, 8192], P('col', 'row'), may hold values from -6 to 6
- weight: bfloat16 [8192, 16384], P('row', 'col'), may hold values from -0.0625 to 0.0625
- feature_bias: float32 [16384], P('col'), may hold values from -3 to 3
- covariance: float32 [16384, 16384], P('row', 'col'), may hold values from -0.5 to 2.5, as said below
- prior_mean: float32 [16384], P('row'), may hold values from -6 to 6
- rewards: float32 [128], replicated, may hold values from -12 to 12
Outputs:
- posterior_cov: float32 [16384, 16384], P('row', 'col')
- posterior_mean: float32 [16384], P('row')
Inputs may be any that keep to these rules, and one draw needn't show every extreme that they name: covariance is exactly symmetric and positive definite.
All inputs are finite; a program needn't handle non-finite values.
Results may differ from a plain program's by a relative error of at most 0.00042.
Values may be sent and summed in bfloat16 or wider, within the bound.
A program may use at most 64 MiB of HBM per device.

v0:
```python
import jax
import jax.numpy as jnp
from jax import lax
from jax.sharding import PartitionSpec as P


def joined_along(blocks, dim):
    dims = list(blocks.shape[1:])
    dims[dim] *= blocks.shape[0]
    return jnp.moveaxis(blocks, 0, dim).reshape(dims)


def from_everyone(array, axis):
    copies = jnp.broadcast_to(array, (lax.axis_size(axis), *array.shape))
    return lax.all_to_all(copies, axis, split_axis=0, concat_axis=0, tiled=True)


def gather_directly(array, axis, dim):
    return joined_along(from_everyone(array, axis), dim)


def cut_along(array, dim, peers):
    before, after = (array.shape[:dim], array.shape[dim + 1 :])
    return jnp.moveaxis(array.reshape(*before, peers, -1, *after), dim, 0)


def summed_on_arrival(array, axis, dim):
    peers = lax.axis_size(axis)
    blocks = lax.all_to_all(cut_along(array, dim, peers), axis, 0, 0, tiled=True)
    return jnp.sum(blocks, axis=0)


def broadcast(array, axis, root):
    return lax.dynamic_index_in_dim(lax.all_gather(array, axis), root, 0, keepdims=False)


def filled_up(lines, peers):
    spare = -len(lines) % peers
    return jnp.pad(lines, [(0, spare)] + [(0, 0)] * (lines.ndim - 1))


def total_of(array, axes):
    lines = array.reshape(-1, array.shape[-1])
    padded = filled_up(lines, lax.axis_size(axes))
    whole = gather_directly(summed_on_arrival(padded, axes, 0), axes, 0)
    return lax.slice_in_dim(whole, 0, len(lines)).reshape(array.shape)


def sum_by_parts(array, axes):
    padded = filled_up(array, lax.axis_size(axes))
    whole = gather_directly(summed_on_arrival(padded, axes, 0), axes, 0)
    return lax.slice_in_dim(whole, 0, len(array)).reshape(array.shape)


def in_one(arrays, axis):
    line, at, outs = (jnp.concatenate([a.reshape(-1) for a in arrays]), 0, [])
    total = sum_by_parts(line, axis)
    for a in arrays:
        outs.append(total[at : at + a.size].reshape(a.shape))
        at += a.size
    return tuple(outs)


def per_device(context, weight, feature_bias, covariance, prior_mean, rewards):
    highest = lax.Precision.HIGHEST
    group_ratio = lax.axis_size("row") // lax.axis_size("col")
    row_index = lax.axis_index("row")
    col_index = lax.axis_index("col")
    row_width = covariance.shape[0]
    tokens = gather_directly(context, "col", 0)
    partial_value = jnp.dot(tokens, weight, preferred_element_type=jnp.float32)
    summed = summed_on_arrival(partial_value, "row", 0)
    features = jnp.tanh(summed + feature_bias[None, :]).astype(jnp.bfloat16)
    phi_col = gather_directly(features, "row", 0)
    phi_held = broadcast(phi_col, "col", row_index // group_ratio)
    phi_row = lax.dynamic_slice_in_dim(phi_held, row_index % group_ratio * row_width, row_width, 1)
    col32 = phi_col.astype(jnp.float32)
    row32 = phi_row.astype(jnp.float32)
    panel_part = jnp.einsum("ik,bk->ib", covariance, col32, precision=highest)
    mean_part = jnp.dot(row32, prior_mean, precision=highest)
    panel = total_of(panel_part, "col")
    gram_part = jnp.dot(row32, panel, precision=highest)
    gram_matrix, predicted = in_one((gram_part, mean_part), "row")
    order = gram_matrix.shape[0]
    gram_matrix = gram_matrix + jnp.eye(order, dtype=jnp.float32)
    lower_factor = jnp.linalg.cholesky(gram_matrix)
    lower_inverse = lax.linalg.triangular_solve(
        lower_factor, jnp.eye(order, dtype=jnp.float32), left_side=True, lower=True
    )
    inverse_gram = jnp.dot(lower_inverse.T, lower_inverse, precision=highest)
    coeffs = jnp.dot(inverse_gram, rewards - predicted, precision=highest)
    gain_rows = jnp.dot(panel, inverse_gram, precision=highest)
    posterior_mean = prior_mean + jnp.dot(panel, coeffs, precision=highest)
    pieces = []
    for member in range(group_ratio):
        pieces.append(broadcast(panel, "row", col_index * group_ratio + member))
    far_panel = jnp.concatenate(pieces, 0)
    update = jnp.einsum("ib,jb->ij", gain_rows, far_panel, precision=highest)
    posterior_cov = covariance - update
    return (posterior_cov, posterior_mean)


def solution(mesh):
    return jax.shard_map(
        per_device,
        mesh=mesh,
        in_specs=(P("col", "row"), P("row", "col"), P("col"), P("row", "col"), P("row"), P()),
        out_specs=(P("row", "col"), P("row")),
        check_vma=False,
    )
```

profile of v0, /device:TPU:1, one launch (start us, length us, event | category | flops | bytes accessed | tf_op | source)
XLA Modules:
  0.0 252.1 jit_solution(7447191661169597824)
XLA Ops:
  7.2 0.7 broadcast_in_dim.15
  8.0 13.9 %all_to_all.40 = bf16[16,8,256]{2,1,0:T(8,128)(2,1)S(1)} all-to-all(bf16[16,8,256]{2,1,0:T(8,128)(2,1)S(1)} %broadcast_in_dim.15), channel_id=1, replica_groups=mesh['row'=32,'col'=16] {'col'}, dimensions={0} | all-to-all | bytes 131072 | tf_op jit(solution)/shard_map/all_to_all | solution.py:15
  21.9 0.2 fusion.3
  22.1 0.3 copy.21
  22.5 50.8 %all_to_all.41 = f32[32,4,1024]{2,1,0:T(4,128)S(1)} all-to-all(f32[32,4,1024]{2,1,0:T(4,128)S(1)} %copy.21), channel_id=1, replica_groups=mesh['row'=32,'col'=16] {'row'}, dimensions={0} | all-to-all | bytes 1048576 | tf_op jit(solution)/shard_map/all_to_all | solution.py:29
  73.5 24.8 %all_to_all.42 = bf16[32,4,1024]{2,1,0:T(4,128)(2,1)S(1)} all-to-all(bf16[32,4,1024]{2,1,0:T(4,128)(2,1)S(1)} %broadcast_in_dim.16), channel_id=1, replica_groups=mesh['row'=32,'col'=16] {'row'}, dimensions={0} | all-to-all | bytes 524288 | tf_op jit(solution)/shard_map/all_to_all | solution.py:15
  98.3 0.8 all_gather_reshape.7
  99.2 1.3 convolution_bitcast_fusion.1
  100.6 10.5 %all_to_all.43 = f32[16,32,128]{2,1,0:T(8,128)S(1)} all-to-all(f32[16,32,128]{2,1,0:T(8,128)S(1)} %bitcast.54), channel_id=1, replica_groups=mesh['row'=32,'col'=16] {'col'}, dimensions={0} | all-to-all | bytes 524288 | tf_op jit(solution)/shard_map/all_to_all | solution.py:29
  111.1 11.2 %all_to_all.44 = f32[16,32,128]{2,1,0:T(8,128)} all-to-all(f32[16,32,128]{2,1,0:T(8,128)S(1)} %broadcast_in_dim.17), channel_id=1, replica_groups=mesh['row'=32,'col'=16] {'col'}, dimensions={0} | all-to-all | bytes 524288 | tf_op jit(solution)/shard_map/all_to_all | solution.py:15
  122.3 33.7 %all-gather.3.cloned.1.call-done = bf16[16,128,1024]{2,1,0:T(8,128)(2,1)} async-done(((bf16[1,128,1024]{2,1,0:T(8,128)(2,1)}), bf16[16,128,1024]{2,1,0:T(8,128)(2,1)}) %all-gather.3.cloned.1.call-update) | async-done | bytes 4194320 | tf_op jit(solution)/shard_map/all_gather | solution.py:34
  156.1 1.1 convolution_bitcast_fusion.2
  157.2 1.4 convolution_bitcast_fusion
  158.6 0.2 all_to_all.30
  158.8 26.8 %all_to_all.45 = f32[32,1,516]{2,1,0:T(1,128)S(1)} all-to-all(f32[32,1,516]{2,1,0:T(1,128)S(1)} %all_to_all.30), channel_id=1, replica_groups=mesh['row'=32,'col'=16] {'row'}, dimensions={0} | all-to-all | bytes 132096 | tf_op jit(solution)/shard_map/all_to_all | solution.py:29
  185.6 0.7 broadcast_in_dim.18
  186.3 5.3 %all-to-all-start.6 = ((f32[32,1,516]{2,1,0:T(1,128)}), f32[32,1,516]{2,1,0:T(1,128)S(1)}, u32[]{:S(2)}, u32[]{:S(2)}) async-start(f32[32,1,516]{2,1,0:T(1,128)} %broadcast_in_dim.18), calls=%async_computation.6 | async-start | bytes 163840 | tf_op jit(solution)/shard_map/all_to_all | solution.py:15
  191.6 15.1 %all-to-all-done.6 = f32[32,1,516]{2,1,0:T(1,128)S(1)} async-done(((f32[32,1,516]{2,1,0:T(1,128)}), f32[32,1,516]{2,1,0:T(1,128)S(1)}, u32[]{:S(2)}, u32[]{:S(2)}) %all-to-all-start.6) | async-done | bytes 66080 | tf_op jit(solution)/shard_map/all_to_all | solution.py:15
  206.7 0.2 reduce.7
  207.3 11.7 %cholesky.18 = f32[128,128]{1,0:T(8,128)S(1)} custom-call(f32[128,128]{1,0:T(8,128)S(1)} %fusion.12), custom_call_target="Cholesky" | custom-call | tf_op jit(solution)/shard_map/jit(cholesky)/cholesky | solution.py:86
  219.1 0.6 compare_reduce_fusion
  219.7 0.7 fusion.9
  220.4 9.8 %custom-call.6 = f32[1,128,128]{1,2,0:T(8,128)S(1)} custom-call(f32[1,128,128]{2,1,0:T(8,128)S(1)} %fusion.9), custom_call_target="InvertDiagBlocksLowerTriangular" | custom-call | tf_op jit(solution)/shard_map/triangular_solve | solution.py:87
  230.2 0.2 fusion.10
  230.5 0.3 fusion.19
  230.8 0.2 convolution_bitcast_fusion.3
  230.9 0.4 fusion.21
  231.3 0.6 add.62
  231.9 0.4 fusion.20
  232.3 8.7 %all-gather.5.cloned.1.call-done = f32[32,512,128]{2,1,0:T(8,128)} async-done(((f32[1,512,128]{2,1,0:T(8,128)}), f32[32,512,128]{2,1,0:T(8,128)}) %all-gather.5.cloned.1.call-update) | async-done | bytes 8388624 | tf_op jit(solution)/shard_map/all_gather | solution.py:34
  241.0 1.1 dynamic-slice_bitcast_fusion.1
  242.1 3.1 %convolution_subtract_fusion = f32[512,1024]{1,0:T(8,128)} fusion(f32[512,1024]{1,0:T(8,128)S(1)} %copy-done.1, f32[512,128]{1,0:T(8,128)S(1)} %fusion.20, f32[512,128]{1,0:T(8,128)S(1)} %get-tuple-element.3, f32[512,128]{1,0:T(8,128)S(1)} %get-tuple-element.2), kind=kOutput, calls=%fused_computation.1 | convolution fusion | flops 805961728 | bytes 4980736 | tf_op jit(solution)/shard_map/ib,jb->ij/dot_general | solution.py:98
  (32 shorter events, 1.1 us)
Async XLA Ops:
  7.2 14.7 %copy-start = (bf16[256,1024]{1,0:T(8,128)(2,1)S(1)}, bf16[256,1024]{1,0:T(8,128)(2,1)}, u32[]{:S(2)}) copy-start(bf16[256,1024]{1,0:T(8,128)(2,1)} %param.7) | copy-start | bytes 1572868
  7.2 66.2 %copy-start.4 = (f32[1024]{0:T(1024)S(1)}, f32[1024]{0:T(1024)}, u32[]{:S(2)}) copy-start(f32[1024]{0:T(1024)} %param.8) | copy-start | bytes 12292
  7.2 148.9 %all-gather.3.cloned.1.call-start = ((), (), s32[]{:S(2)}) async-start(), calls=%async_computation.7 | async-start | bytes 4456448 | tf_op jit(solution)/shard_map/all_gather | solution.py:34
  22.5 76.7 %copy-start.1 = (f32[512,1024]{1,0:T(8,128)S(1)}, f32[512,1024]{1,0:T(8,128)}, u32[]{:S(2)}) copy-start(f32[512,1024]{1,0:T(8,128)} %param.9) | copy-start | bytes 6291460
  99.1 142.0 %all-gather.5.cloned.1.call-start = ((), (), s32[]{:S(2)}) async-start(), calls=%async_computation.8 | async-start | bytes 8650752 | tf_op jit(solution)/shard_map/all_gather | solution.py:34
  99.2 56.9 %copy-start.3 = (f32[512]{0:T(512)S(1)}, f32[512]{0:T(512)}, u32[]{:S(2)}) copy-start(f32[512]{0:T(512)} %param.10) | copy-start | bytes 6148
  111.1 119.7 %copy-start.5 = (f32[128]{0:T(128)S(1)}, f32[128]{0:T(128)}, u32[]{:S(2)}) copy-start(f32[128]{0:T(128)} %param.11) | copy-start | bytes 1540
  122.3 108.7 %copy-start.2 = (f32[16,32,128]{2,1,0:T(8,128)S(1)}, f32[16,32,128]{2,1,0:T(8,128)}, u32[]{:S(2)}) copy-start(f32[16,32,128]{2,1,0:T(8,128)} %all_to_all.44) | copy-start | bytes 786436
  186.3 20.4 %all-to-all-start.6 = ((f32[32,1,516]{2,1,0:T(1,128)}), f32[32,1,516]{2,1,0:T(1,128)S(1)}, u32[]{:S(2)}, u32[]{:S(2)}) async-start(f32[32,1,516]{2,1,0:T(1,128)} %broadcast_in_dim.18), calls=%async_computation.6 | async-start | bytes 163840 | tf_op jit(solution)/shard_map/all_to_all | solution.py:15
Sparse Core Ops, SparseCore 0:
  99.2 56.8 all-gather.2
  158.2 82.8 all-gather.4
where the time goes:
time: 253 us; the launch traced here: 252 us
  blocking collectives  138 us (55%)
  waiting for transfers between devices  57.6 us (23%)
  other arithmetic  23.9 us (9%)
  between operations  14.3 us (6%)
  matrix products  8.6 us (3%)
  starting transfers between devices  5.35 us (2%)
  local copies, waits for them, and re-layouts  4.45 us (2%)
    all_to_all x3, blocking collectives, summed_on_arrival(): lax.all_to_all(cut_along(array, dim, peers), axis, 0, 0, tiled=True)  88 us
    all_to_all x3, blocking collectives, from_everyone(): return lax.all_to_all(copies, axis, split_axis=0, concat_axis=0, tiled=True)  49.8 us
    all_gather x2, waiting for transfers between devices, broadcast(): lax.all_gather(array, axis)  42.5 us
    all_to_all x1, waiting for transfers between devices, from_everyone(): return lax.all_to_all(copies, axis, split_axis=0, concat_axis=0, tiled=True)  15.1 us
    another operation x3, other arithmetic, per_device(): lower_factor = jnp.linalg.cholesky(gram_matrix)  12.4 us
    another operation x2, other arithmetic, per_device(): lax.linalg.triangular_solve(lower_factor, jnp.eye(order, dtype=jnp.float3...  10.5 us
    all_to_all x1, starting transfers between devices, from_everyone(): return lax.all_to_all(copies, axis, split_axis=0, concat_axis=0, tiled=True)  5.27 us
  transfers between devices with their start and end apart: 3, of which 3 were waited for; matrix products, arithmetic and copies ran while one was open for 12% of the time, Pallas kernels for 0%

commit v1 on v0

v1 whole, which is shorter than its diff:
```python
import jax, jax.numpy as jnp
from jax import lax
from jax.experimental import pallas as pl
from jax.experimental.pallas import tpu as pltpu

HI = lax.Precision.HIGHEST


def split3(x):
    hi = x.astype(jnp.bfloat16)
    rest = x - hi.astype(jnp.float32)
    mid = rest.astype(jnp.bfloat16)
    lo = (rest - mid.astype(jnp.float32)).astype(jnp.bfloat16)
    return hi, mid, lo


def sweep_inverse(a):
    n = a.shape[0]
    lane = lax.broadcasted_iota(jnp.int32, (8, n), 1)
    sub = lax.broadcasted_iota(jnp.int32, (8, 1), 0)
    blocks = [a[8 * i : 8 * i + 8] for i in range(n // 8)]
    for j in range(n):
        at, s = j // 8, j % 8
        mine = blocks[at]
        pivot = 1.0 / mine[s : s + 1, j : j + 1]
        in_lane = lane == j
        row = jnp.where(in_lane[:1], 1.0, mine[s : s + 1]) * pivot
        row = jnp.broadcast_to(row, (8, n))
        new = []
        for i, block in enumerate(blocks):
            col = block[:, j : j + 1]
            kept = jnp.where(in_lane, 0.0, block)
            if i == at:
                col = jnp.where(sub == s, -1.0, col)
                kept = jnp.where(sub == s, 0.0, kept)
            new.append(kept - col * row)
        blocks = new
    return jnp.concatenate(blocks, 0)


def update_kernel(g_ref, pred_ref, rew_ref, mean_ref, pr_ref, pc_ref, cov_ref, out_ref, outm_ref, gain_s, pc_s):
    step = pl.program_id(0)
    rows = cov_ref.shape[0]

    @pl.when(step == 0)
    def _():
        b = g_ref.shape[0]
        eye = (lax.broadcasted_iota(jnp.int32, (b, b), 0) == lax.broadcasted_iota(jnp.int32, (b, b), 1)).astype(jnp.float32)
        inv = sweep_inverse(g_ref[...] + eye)
        diff = rew_ref[...] - pred_ref[...]
        coeffs = jnp.dot(jnp.broadcast_to(diff, (8, b)), inv, precision=HI, preferred_element_type=jnp.float32)
        outm_ref[...] = mean_ref[...] + jnp.dot(coeffs, pr_ref[...], precision=HI, preferred_element_type=jnp.float32)[:1]
        gain = jnp.dot(inv, pr_ref[...], precision=HI, preferred_element_type=jnp.float32)
        hi, mid, _ = split3(gain)
        for i in range(gain_s.shape[0]):
            cut = slice(i * rows, i * rows + rows)
            gain_s[i] = jnp.concatenate([hi[:, cut], hi[:, cut], mid[:, cut]], 0)
        phi, pmid, _ = split3(pc_ref[...])
        pc_s[...] = jnp.concatenate([phi, pmid, phi], 0)

    update = lax.dot_general(gain_s[step], pc_s[...], (((0,), (0,)), ((), ())), preferred_element_type=jnp.float32)
    out_ref[...] = cov_ref[...] - update


def update(g, pred, rew, mean, pr, pc, cov, steps=4):
    b = g.shape[0]
    n, m = cov.shape
    rows = n // steps
    whole = lambda *shape: pl.BlockSpec(shape, lambda i: (0, 0))
    return pl.pallas_call(
        update_kernel,
        grid=(steps,),
        in_specs=[whole(b, b), whole(1, b), whole(1, b), whole(1, n), whole(b, n), whole(b, m), pl.BlockSpec((rows, m), lambda i: (i, 0))],
        out_specs=[pl.BlockSpec((rows, m), lambda i: (i, 0)), whole(1, n)],
        out_shape=[jax.ShapeDtypeStruct((n, m), jnp.float32), jax.ShapeDtypeStruct((1, n), jnp.float32)],
        scratch_shapes=[pltpu.VMEM((steps, 3 * b, rows), jnp.bfloat16), pltpu.VMEM((3 * b, m), jnp.bfloat16)],
    )(g, pred, rew, mean, pr, pc, cov)
from jax.sharding import PartitionSpec as P

MESH = pl.DeviceIdType.MESH


def far_first(t, n):
    return n // 2 + (1 - 2 * (t % 2)) * ((t + 1) // 2)


def near_first(t, n):
    return far_first(n - 2 - t, n)


def exchange_kernel(
    ctx_hbm, w_hbm, bias_hbm, cov_hbm, mean_hbm,
    g_out, pred_out, pr_out, pc_out,
    ctx_all, ctx_m, w_v, bias_v, cov_v, mean_v, c_hi, c_mid, c_lo,
    x_send, x_recv, z_send, z_recv, phi_s, phi_c, phi_p, phi_r,
    pp_send, pp_recv, p_own, g_send, g_recv, gz_s, gz_r, pz_s, pz_r, g_s, g_all,
    pr_all, p_z, pc_all,
    local, near, pair_s, pair_r, send, recv, mate,
):
    nz, nc, nb = z_send.shape[0], ctx_all.shape[0], 4
    r, c = lax.axis_index("row"), lax.axis_index("col")
    z, h = r // 2, r % 2
    other = 1 - h

    def at(zz, hh, cc):
        return (zz * 2 + hh, cc)

    def remote(src, dst, s_sem, r_sem, where):
        return pltpu.make_async_remote_copy(
            src_ref=src, dst_ref=dst, send_sem=s_sem, recv_sem=r_sem, device_id=where, device_id_type=MESH
        )

    loads = [
        pltpu.make_async_copy(ctx_hbm, ctx_all.at[c], local.at[0]),
        pltpu.make_async_copy(cov_hbm, cov_v, local.at[1]),
        pltpu.make_async_copy(w_hbm, w_v, local.at[2]),
        pltpu.make_async_copy(bias_hbm, bias_v, local.at[3]),
        pltpu.make_async_copy(mean_hbm, mean_v, local.at[4]),
    ]
    for load in loads:
        load.start()

    barrier = pltpu.get_barrier_semaphore()

    def greet(where):
        pl.semaphore_signal(barrier, inc=1, device_id=where, device_id_type=MESH)

    def greet_plane(t, _):
        greet(at(z, h, (c + t) % nc))
        return 0

    def greet_line(t, _):
        greet(at((z + t) % nz, h, c))
        greet(at((z - t + nz) % nz, h, c))
        greet(at((z + t) % nz, other, c))
        greet(at((z - t + nz) % nz, other, c))
        return 0

    lax.fori_loop(1, nc, greet_plane, 0)
    lax.fori_loop(1, nb + 1, greet_line, 0)
    greet(at(z, other, c))
    pl.semaphore_wait(barrier, nc - 1 + 4 * nb + 1)
    pl.semaphore_signal(near, inc=1, device_id=at((z + nb) % nz, h, c), device_id_type=MESH)
    pl.semaphore_signal(near, inc=1, device_id=at((z - nb + nz) % nz, h, c), device_id_type=MESH)

    def ctx_copy(t):
        return remote(ctx_hbm, ctx_all.at[c], send.at[0, t], recv.at[0, c], at(z, h, (c + t) % nc))

    def plane_arrival(buf, phase, src):
        return remote(buf.at[src], buf.at[src], send.at[phase, 0], recv.at[phase, src], at(z, other, c))

    def start_ctx(t, _):
        ctx_copy(t).start()
        return 0

    lax.fori_loop(1, nc, start_ctx, 0)

    loads[1].wait()
    rows = cov_v.shape[0]

    def split_cov(i, _):
        cut = pl.ds(pl.multiple_of(i * 64, 64), 64)
        hi, mid, lo = split3(cov_v[cut, :])
        c_hi[cut, :] = hi
        c_mid[cut, :] = mid
        c_lo[cut, :] = lo
        return 0

    lax.fori_loop(0, rows // 64, split_cov, 0)
    loads[2].wait()
    loads[3].wait()
    loads[4].wait()
    loads[0].wait()

    def wait_ctx(t, _):
        plane_arrival(ctx_all, 0, (c + t) % nc).wait_recv()
        return 0

    lax.fori_loop(1, nc, wait_ctx, 0)
    tokens, depth = ctx_m.shape
    half = tokens // 2
    ctx_m[...] = ctx_all[...].astype(jnp.float32).reshape(tokens, depth).astype(jnp.bfloat16)

    theirs = ctx_m[pl.ds(pl.multiple_of(other * half, half), half), :]
    x_send[...] = jnp.dot(theirs, w_v[...], preferred_element_type=jnp.float32)
    swap_x = remote(x_send, x_recv, pair_s.at[0], pair_r.at[0], at(z, other, c))
    swap_x.start()
    mine = ctx_m[pl.ds(pl.multiple_of(h * half, half), half), :]
    own = jnp.dot(mine, w_v[...], preferred_element_type=jnp.float32)
    z_pieces = [(slice(k // 4 * 16, k // 4 * 16 + 16), slice(k % 4 * 256, k % 4 * 256 + 256)) for k in range(nz)]
    for k, (a, b) in enumerate(z_pieces):
        z_send[k] = own[a, b]
    swap_x.wait_recv()
    for k, (a, b) in enumerate(z_pieces):
        z_send[k] += x_recv[a, b]
    pl.semaphore_wait(near, 2)

    def line_copy(src, dst, phase, t):
        return remote(src, dst, send.at[phase, t], recv.at[phase, z], at((z + t) % nz, h, c))

    def line_arrival(buf, phase, src):
        return remote(buf.at[src], buf.at[src], send.at[phase, 0], recv.at[phase, src], at(z, other, c))

    def start_z(t, _):
        t = far_first(t, nz)
        line_copy(z_send.at[(z + t) % nz], z_recv.at[z], 1, t).start()
        return 0

    lax.fori_loop(0, nz - 1, start_z, 0)
    z_recv[z] = z_send[z]

    def wait_z(t, _):
        line_arrival(z_recv, 1, (z + t) % nz).wait_recv()
        return 0

    lax.fori_loop(1, nz, wait_z, 0)
    kb = z % 4
    total = jnp.sum(z_recv[...], axis=0) + bias_v[:, pl.ds(pl.multiple_of(kb * 256, 256), 256)]
    phi = jnp.tanh(total).astype(jnp.bfloat16)
    phi_s[...] = phi

    def start_phi(t, _):
        t = far_first(t, nz)
        line_copy(phi_s, phi_c.at[h * nz + z], 2, t).start()
        return 0

    lax.fori_loop(0, nz - 1, start_phi, 0)

    def mate_copy(k):
        return remote(phi_c.at[h * nz + k], phi_c.at[h * nz + k], mate.at[0, k], mate.at[1, k], at(z, other, c))

    phi_c[h * nz + z] = phi
    mate_copy(z).start()

    def plane_copy(src, dst, phase, t):
        return remote(src, dst, send.at[phase, t], recv.at[phase, c], at(z, h, (c + t) % nc))

    def start_plane_phi(t, _):
        plane_copy(phi_s, phi_p.at[c], 3, t).start()
        return 0

    lax.fori_loop(1, nc, start_plane_phi, 0)
    phi_p[c] = phi

    goal = kb // 2
    slot = h * 8 + z // 4 * 2 + kb % 2

    def row_copy(t):
        zz = (c + t) % nc
        return remote(phi_p.at[zz], phi_r.at[slot], send.at[4, t], recv.at[4, slot], at(zz, goal, c))

    def pass_phi(t, _):
        zz = (c + t) % nc

        @pl.when(t > 0)
        def _():
            plane_arrival(phi_p, 3, zz).wait_recv()

        here = jnp.logical_and(zz == z, goal == h)

        @pl.when(here)
        def _():
            phi_r[slot] = phi_p[zz]

        @pl.when(jnp.logical_not(here))
        def _():
            row_copy(t).start()

        return 0

    lax.fori_loop(0, nc, pass_phi, 0)

    def pass_mate(t, _):
        zz = (z + near_first(t, nz)) % nz
        remote(phi_s, phi_c.at[h * nz + zz], send.at[2, 0], recv.at[2, zz], at(z, other, c)).wait_recv()
        mate_copy(zz).start()
        return 0

    lax.fori_loop(0, nz - 1, pass_mate, 0)

    def wait_mate(t, _):
        k = other * nz + t
        remote(phi_c.at[k], phi_c.at[k], mate.at[0, t], mate.at[1, t], at(z, other, c)).wait_recv()
        return 0

    lax.fori_loop(0, nz, wait_mate, 0)

    part = None
    for k in range(4):
        lhs = jnp.concatenate([phi_c[i * 4 + k] for i in range(8)], 0)
        for term in (c_hi, c_mid, c_lo):
            prod = lax.dot_general(
                lhs, term[:, k * 256 : k * 256 + 256], (((1,), (1,)), ((), ())), preferred_element_type=jnp.float32
            )
            part = prod if part is None else part + prod
    pp_send[...] = part.reshape(pp_send.shape)

    def start_pp(t, _):
        plane_copy(pp_send.at[(c + t) % nc], pp_recv.at[c], 5, t).start()
        return 0

    lax.fori_loop(1, nc, start_pp, 0)
    pp_recv[c] = pp_send[c]

    def source_here(s):
        zz = s % 8 // 2 * 4 + goal_of(s)
        return jnp.logical_and(zz == z, s // 8 == h)

    def goal_of(s):
        return 2 * h + s % 2

    def wait_row(s, _):
        @pl.when(jnp.logical_not(source_here(s)))
        def _():
            plane_arrival(phi_r, 4, s).wait_recv()

        return 0

    lax.fori_loop(0, nz, wait_row, 0)

    def wait_pp(t, _):
        plane_arrival(pp_recv, 5, (c + t) % nc).wait_recv()
        return 0

    lax.fori_loop(1, nc, wait_pp, 0)
    p_mine = jnp.sum(pp_recv[...], axis=0)
    p_own[...] = p_mine

    def start_pr(t, _):
        plane_copy(p_own, pr_all.at[c], 6, t).start()
        return 0

    lax.fori_loop(1, nc, start_pr, 0)
    pr_all[c] = p_mine
    p_z[z] = p_mine

    width = p_mine.shape[1]
    zeros = jnp.zeros((7, width), jnp.float32)
    terms = split3(jnp.concatenate([p_mine, mean_v[...], zeros], 0))
    stacked = jnp.concatenate(terms, 0)
    gram = None
    for k in range(2):
        rhs = jnp.concatenate([phi_r[i * 2 + k] for i in range(8)], 0)
        prod = lax.dot_general(
            stacked[:, k * 256 : k * 256 + 256], rhs, (((1,), (1,)), ((), ())), preferred_element_type=jnp.float32
        )
        gram = prod if gram is None else gram + prod
    g_send[...] = gram[:16] + gram[16:32] + gram[32:]
    swap_g = remote(g_send, g_recv, pair_s.at[1], pair_r.at[1], at(z, other, c))
    swap_g.start()
    swap_g.wait_recv()
    both = g_send[...] + g_recv[...]
    gz_s[...] = both[:8]
    pz_s[...] = both[8:9]

    def start_gz(t, _):
        t = far_first(t, nz)
        line_copy(gz_s, gz_r.at[z], 7, t).start()
        line_copy(pz_s, pz_r.at[z], 8, t).start()
        return 0

    lax.fori_loop(0, nz - 1, start_gz, 0)
    gz_r[z] = both[:8]
    pz_r[z] = both[8:9]

    def start_pz(t, _):
        t = far_first(t, nz)
        line_copy(p_own, p_z.at[z], 9, t).start()
        return 0

    lax.fori_loop(0, nz - 1, start_pz, 0)

    def wait_gz(t, _):
        zz = (z + t) % nz
        line_arrival(gz_r, 7, zz).wait_recv()
        line_arrival(pz_r, 8, zz).wait_recv()
        return 0

    lax.fori_loop(1, nz, wait_gz, 0)
    g_rows = jnp.sum(gz_r[...], axis=0)
    g_s[...] = g_rows

    def start_g(t, _):
        plane_copy(g_s, g_all.at[c], 10, t).start()
        return 0

    lax.fori_loop(1, nc, start_g, 0)
    g_all[c] = g_rows
    pred_out[...] = jnp.sum(pz_r[...], axis=0)

    def col_copy(zz):
        return remote(p_z.at[zz], pc_all.at[h, c], send.at[11, zz], recv.at[11, c], at(z, h, zz))

    def pass_pz(t, _):
        zz = (z + t) % nz

        @pl.when(t > 0)
        def _():
            line_arrival(p_z, 9, zz).wait_recv()

        @pl.when(zz == c)
        def _():
            pc_all[h, c] = p_z[zz]

        @pl.when(zz != c)
        def _():
            col_copy(zz).start()

        return 0

    lax.fori_loop(0, nz, pass_pz, 0)

    def mate_pc(p):
        return remote(pc_all.at[h, p], pc_all.at[h, p], mate.at[2, p], mate.at[3, p], at(z, other, c))

    def pass_pc(t, _):
        p = (c + t) % nc

        @pl.when(t > 0)
        def _():
            remote(p_own, pc_all.at[h, p], send.at[11, 0], recv.at[11, p], at(z, other, c)).wait_recv()

        mate_pc(p).start()
        return 0

    lax.fori_loop(0, nc, pass_pc, 0)

    def wait_last(t, _):
        p = (c + t) % nc
        plane_arrival(pr_all, 6, p).wait_recv()
        plane_arrival(g_all, 10, p).wait_recv()
        return 0

    lax.fori_loop(1, nc, wait_last, 0)
    g_out[...] = g_all[...].reshape(g_out.shape)
    pr_out[...] = pr_all[...].reshape(pr_out.shape)

    def wait_pc(p, _):
        remote(p_own, pc_all.at[other, p], mate.at[2, p], mate.at[3, p], at(z, other, c)).wait_recv()
        return 0

    lax.fori_loop(0, nc, wait_pc, 0)
    for k in range(2):
        pc_out[:, k * width : (k + 1) * width] = pc_all[k].reshape(tokens, width)

    swap_x.wait_send()
    swap_g.wait_send()

    def sent(t, _):
        ctx_copy(t).wait_send()
        line_copy(z_send.at[(z + t) % nz], z_recv.at[z], 1, t).wait_send()
        line_copy(phi_s, phi_c.at[h * nz + z], 2, t).wait_send()
        plane_copy(phi_s, phi_p.at[c], 3, t).wait_send()
        plane_copy(pp_send.at[(c + t) % nc], pp_recv.at[c], 5, t).wait_send()
        plane_copy(p_own, pr_all.at[c], 6, t).wait_send()
        line_copy(gz_s, gz_r.at[z], 7, t).wait_send()
        line_copy(pz_s, pz_r.at[z], 8, t).wait_send()
        line_copy(p_own, p_z.at[z], 9, t).wait_send()
        plane_copy(g_s, g_all.at[c], 10, t).wait_send()
        return 0

    lax.fori_loop(1, nz, sent, 0)

    def sent_some(t, _):
        mate_copy(t).wait_send()
        mate_pc(t).wait_send()

        @pl.when(jnp.logical_not(jnp.logical_and((c + t) % nc == z, goal == h)))
        def _():
            row_copy(t).wait_send()

        @pl.when(t != c)
        def _():
            col_copy(t).wait_send()

        return 0

    lax.fori_loop(0, nz, sent_some, 0)


def exchange(context, weight, bias, covariance, mean):
    rows_here, depth = context.shape
    n, m = covariance.shape
    nz, nc = lax.axis_size("row") // 2, lax.axis_size("col")
    b = rows_here * nc
    f32, bf16 = jnp.float32, jnp.bfloat16
    vmem, sem = pltpu.VMEM, pltpu.SemaphoreType
    scratch = [
        vmem((nc, rows_here, depth), bf16), vmem((b, depth), bf16), vmem((depth, m), bf16), vmem((1, m), f32),
        vmem((n, m), f32), vmem((1, n), f32), vmem((n, m), bf16), vmem((n, m), bf16), vmem((n, m), bf16),
        vmem((b // 2, m), f32), vmem((b // 2, m), f32), vmem((nz, 16, 256), f32), vmem((nz, 16, 256), f32),
        vmem((16, 256), bf16), vmem((2 * nz, 16, 256), bf16), vmem((nc, 16, 256), bf16), vmem((16, 16, 256), bf16),
        vmem((nc, 8, n), f32), vmem((nc, 8, n), f32), vmem((8, n), f32), vmem((16, b), f32), vmem((16, b), f32),
        vmem((8, b), f32), vmem((nz, 8, b), f32), vmem((1, b), f32), vmem((nz, 1, b), f32), vmem((8, b), f32), vmem((nc, 8, b), f32),
        vmem((nc, 8, n), f32), vmem((nz, 8, n), f32), vmem((2, nc, 8, n), f32),
        sem.DMA((5,)), sem.REGULAR, sem.DMA((2,)), sem.DMA((2,)), sem.DMA((12, 16)), sem.DMA((12, 16)), sem.DMA((4, 16)),
    ]
    return pl.pallas_call(
        exchange_kernel,
        in_specs=[pl.BlockSpec(memory_space=pl.ANY)] * 5,
        out_specs=[pl.BlockSpec(memory_space=pltpu.VMEM)] * 4,
        out_shape=[jax.ShapeDtypeStruct(s, f32) for s in ((b, b), (1, b), (b, n), (b, m))],
        scratch_shapes=scratch,
        compiler_params=pltpu.CompilerParams(collective_id=0, has_side_effects=True),
    )(context, weight, bias, covariance, mean)


def per_device(context, weight, feature_bias, covariance, prior_mean, rewards):
    mean = prior_mean.reshape(1, -1)
    g, pred, pr, pc = exchange(context, weight, feature_bias.reshape(1, -1), covariance, mean)
    cov, mean = update(g, pred, rewards.reshape(1, -1), mean, pr, pc, covariance)
    return cov, mean.reshape(-1)


def solution(mesh):
    return jax.shard_map(
        per_device,
        mesh=mesh,
        in_specs=(P("col", "row"), P("row", "col"), P("col"), P("row", "col"), P("row"), P()),
        out_specs=(P("row", "col"), P("row")),
        check_vma=False,
    )
```

time: 253 us -> 100 us (0.40)
  the two profiles are of different devices: /device:TPU:1 before, /device:TPU:33 now
where the time goes in v1:
time: 100 us
  Pallas kernels  99.3 us (99%)
    pallas_call x1, Pallas kernels, exchange(): pl.pallas_call(exchange_kernel, in_specs=[pl.BlockSpec(memory_space=pl.AN...  83 us
    pallas_call x1, Pallas kernels, update(): pl.pallas_call(update_kernel, grid=(steps,), in_specs=[whole(b, b), whole...  16.3 us

profile of v1, /device:TPU:33, one launch (start us, length us, event | category | flops | bytes accessed | tf_op | source)
XLA Modules:
  0.0 100.0 jit_solution(12189521621156667405)
XLA Ops:
  0.6 83.0 %shard_map.77 = (f32[128,128]{1,0:T(8,128)}, f32[1,128]{1,0:T(1,128)}, f32[128,512]{1,0:T(8,128)}, f32[128,1024]{1,0:T(8,128)}) custom-call(bf16[8,256]{1,0:T(8,128)(2,1)} %ctx_hbm.1, bf16[256,1024]{1,0:T(8,128)(2,1)} %w_hbm.1, f32[1,1024]{1,0:T(1,128)} %bitcast.6, f32[512,1024]{1,0:T(8,128)} %cov_ref.1, f32[1,512]{1,0:T(1,128)} %bitcast.4), custom_call_target="tpu_custom_call" | custom-call | tf_op jit(solution)/shard_map/pallas_call | solution.py:498
  83.7 16.3 %shard_map.78 = (f32[512,1024]{1,0:T(8,128)}, f32[1,512]{1,0:T(1,128)}) custom-call(f32[128,128]{1,0:T(8,128)} %get-tuple-element.8.g_ref, f32[1,128]{1,0:T(1,128)} %get-tuple-element.9.pred_ref, f32[1,128]{1,0:T(1,128)} %bitcast.7, f32[1,512]{1,0:T(1,128)} %bitcast.5, f32[128,512]{1,0:T(8,128)} %get-tuple-element.10.pr_ref, ...), custom_call_target="tpu_custom_call" | custom-call | tf_op jit(solution)/shard_map/pallas_call | solution.py:70

commit v2 on v1

--- a/solution.py
+++ b/solution.py
@@ -1,9 +1,12 @@
-import jax, jax.numpy as jnp
+import jax
+import jax.numpy as jnp
 from jax import lax
 from jax.experimental import pallas as pl
 from jax.experimental.pallas import tpu as pltpu
+from jax.sharding import PartitionSpec as P
 
 HI = lax.Precision.HIGHEST
+MESH = pl.DeviceIdType.MESH
 
 
 def split3(x):
@@ -14,27 +17,106 @@
     return hi, mid, lo
 
 
-def sweep_inverse(a):
+def coded_sum(x):
+    t = x * 16.0
+    t2 = t * t
+    t4 = t2 * t2
+    return ((t4 * t4) * t2 * t).astype(jnp.bfloat16)
+
+
+def coded_panel(x):
+    t = x * 4.0
+    t2 = t * t
+    return ((t2 * t2) * t2 * t).astype(jnp.bfloat16)
+
+
+def rooted(y, power, scale):
+    y = y.astype(jnp.float32)
+    v = jnp.exp(jnp.log(jnp.abs(y)) * (1.0 / power)) * (1.0 / scale)
+    return jnp.where(y < 0, -v, v)
+
+
+def sum_from(y):
+    return rooted(y, 11, 16)
+
+
+def panel_from(y):
+    return rooted(y, 7, 4)
+
+
+def inverse_of_2(a, b, c):
+    scale = 1.0 / (a * c - b * b)
+    return c * scale, -b * scale, a * scale
+
+
+def inverse_of_4(m):
+    a0, a1, a2 = inverse_of_2(m[0][0], m[0][1], m[1][1])
+    t = [[a0 * m[0][2 + k] + a1 * m[1][2 + k] for k in range(2)], [a1 * m[0][2 + k] + a2 * m[1][2 + k] for k in range(2)]]
+    s0 = m[2][2] - (m[0][2] * t[0][0] + m[1][2] * t[1][0])
+    s1 = m[2][3] - (m[0][2] * t[0][1] + m[1][2] * t[1][1])
+    s2 = m[3][3] - (m[0][3] * t[0][1] + m[1][3] * t[1][1])
+    c0, c1, c2 = inverse_of_2(s0, s1, s2)
+    u = [[t[i][0] * c0 + t[i][1] * c1, t[i][0] * c1 + t[i][1] * c2] for i in range(2)]
+    b0 = a0 + u[0][0] * t[0][0] + u[0][1] * t[0][1]
+    b1 = a1 + u[0][0] * t[1][0] + u[0][1] * t[1][1]
+    b2 = a2 + u[1][0] * t[1][0] + u[1][1] * t[1][1]
+    return [
+        [b0, b1, -u[0][0], -u[0][1]],
+        [b1, b2, -u[1][0], -u[1][1]],
+        [-u[0][0], -u[1][0], c0, c1],
+        [-u[0][1], -u[1][1], c1, c2],
+    ]
+
+
+def panel4(blocks, lo, lane, sub):
+    n = blocks[0].shape[1]
+    for j in range(lo, lo + 8 * len(blocks), 4):
+        at, s = (j - lo) // 8, j % 8
+        mine = blocks[at]
+        cell = [[None] * 4 for _ in range(4)]
+        for i in range(4):
+            for k in range(i, 4):
+                cell[i][k] = cell[k][i] = jnp.broadcast_to(mine[s + i : s + i + 1, j + k : j + k + 1], (8, n))
+        inv = inverse_of_4(cell)
+        inside = (lane >= j) & (lane < j + 4)
+        rows = [
+            jnp.where(inside, jnp.where(lane == j + m, 1.0, 0.0), jnp.broadcast_to(mine[s + m : s + m + 1], (8, n)))
+            for m in range(4)
+        ]
+        out = [(inv[i][0] * rows[0] + inv[i][1] * rows[1]) + (inv[i][2] * rows[2] + inv[i][3] * rows[3]) for i in range(4)]
+        new = []
+        for i, block in enumerate(blocks):
+            kept = jnp.where(inside, 0.0, block)
+            cols = [jnp.broadcast_to(block[:, j + k : j + k + 1], (8, n)) for k in range(4)]
+            if i == at:
+                here = (sub >= s) & (sub < s + 4)
+                kept = jnp.where(here, 0.0, kept)
+                cols = [jnp.where(here, jnp.where(sub == s + k, -1.0, 0.0), cols[k]) for k in range(4)]
+            new.append(kept - ((cols[0] * out[0] + cols[1] * out[1]) + (cols[2] * out[2] + cols[3] * out[3])))
+        blocks = new
+    return blocks
+
+
+def dot3(a, b):
+    ah, am, al = split3(a)
+    bh, bm, bl = split3(b)
+    return jnp.dot(jnp.concatenate([ah, ah, am, am, ah, al], 1), jnp.concatenate([bh, bm, bh, bm, bl, bh], 0), preferred_element_type=jnp.float32)
+
+
+def spd_inverse(a, w):
     n = a.shape[0]
     lane = lax.broadcasted_iota(jnp.int32, (8, n), 1)
-    sub = lax.broadcasted_iota(jnp.int32, (8, 1), 0)
+    sub = lax.broadcasted_iota(jnp.int32, (8, n), 0)
     blocks = [a[8 * i : 8 * i + 8] for i in range(n // 8)]
-    for j in range(n):
-        at, s = j // 8, j % 8
-        mine = blocks[at]
-        pivot = 1.0 / mine[s : s + 1, j : j + 1]
-        in_lane = lane == j
-        row = jnp.where(in_lane[:1], 1.0, mine[s : s + 1]) * pivot
-        row = jnp.broadcast_to(row, (8, n))
-        new = []
-        for i, block in enumerate(blocks):
-            col = block[:, j : j + 1]
-            kept = jnp.where(in_lane, 0.0, block)
-            if i == at:
-                col = jnp.where(sub == s, -1.0, col)
-                kept = jnp.where(sub == s, 0.0, kept)
-            new.append(kept - col * row)
-        blocks = new
+    for lo in range(0, n, w):
+        first, last = lo // 8, (lo + w) // 8
+        panel = panel4(blocks[first:last], lo, lane, sub)
+        rest = blocks[:first] + blocks[last:]
+        cols = jnp.concatenate([b[:, lo : lo + w] for b in rest], 0)
+        prod = dot3(cols, jnp.concatenate(panel, 0))
+        inside = (lane >= lo) & (lane < lo + w)
+        rest = [jnp.where(inside, 0.0, b) - prod[8 * i : 8 * i + 8] for i, b in enumerate(rest)]
+        blocks = rest[:first] + panel + rest[first:]
     return jnp.concatenate(blocks, 0)
 
 
@@ -45,39 +127,46 @@
     @pl.when(step == 0)
     def _():
         b = g_ref.shape[0]
+        width = pc_ref.shape[-1]
+        for k in range(2):
+            panel = panel_from(pc_ref[k]).reshape(b, width)
+            hi, mid, _ = split3(panel)
+            cut = slice(k * width, k * width + width)
+            pc_s[:b, cut] = hi
+            pc_s[b : 2 * b, cut] = mid
+            pc_s[2 * b :, cut] = hi
+        pr = pr_ref[...]
+        pr_t = pr.T
         eye = (lax.broadcasted_iota(jnp.int32, (b, b), 0) == lax.broadcasted_iota(jnp.int32, (b, b), 1)).astype(jnp.float32)
-        inv = sweep_inverse(g_ref[...] + eye)
+        inv = spd_inverse(g_ref[...] + eye, 16)
+        gain = jnp.dot(pr_t, inv, precision=HI, preferred_element_type=jnp.float32)
+        hi, mid, _ = split3(gain)
+        gain_s[:, :b] = hi
+        gain_s[:, b : 2 * b] = hi
+        gain_s[:, 2 * b :] = mid
         diff = rew_ref[...] - pred_ref[...]
         coeffs = jnp.dot(jnp.broadcast_to(diff, (8, b)), inv, precision=HI, preferred_element_type=jnp.float32)
-        outm_ref[...] = mean_ref[...] + jnp.dot(coeffs, pr_ref[...], precision=HI, preferred_element_type=jnp.float32)[:1]
-        gain = jnp.dot(inv, pr_ref[...], precision=HI, preferred_element_type=jnp.float32)
-        hi, mid, _ = split3(gain)
-        for i in range(gain_s.shape[0]):
-            cut = slice(i * rows, i * rows + rows)
-            gain_s[i] = jnp.concatenate([hi[:, cut], hi[:, cut], mid[:, cut]], 0)
-        phi, pmid, _ = split3(pc_ref[...])
-        pc_s[...] = jnp.concatenate([phi, pmid, phi], 0)
-
-    update = lax.dot_general(gain_s[step], pc_s[...], (((0,), (0,)), ((), ())), preferred_element_type=jnp.float32)
-    out_ref[...] = cov_ref[...] - update
+        outm_ref[...] = mean_ref[...] + jnp.dot(coeffs, pr, precision=HI, preferred_element_type=jnp.float32)[:1]
+
+    mine = gain_s[pl.ds(pl.multiple_of(step * rows, rows), rows), :]
+    out_ref[...] = cov_ref[...] - jnp.dot(mine, pc_s[...], preferred_element_type=jnp.float32)
 
 
 def update(g, pred, rew, mean, pr, pc, cov, steps=4):
     b = g.shape[0]
     n, m = cov.shape
     rows = n // steps
-    whole = lambda *shape: pl.BlockSpec(shape, lambda i: (0, 0))
+    whole = lambda *shape: pl.BlockSpec(shape, lambda i: (0,) * len(shape))
     return pl.pallas_call(
         update_kernel,
         grid=(steps,),
-        in_specs=[whole(b, b), whole(1, b), whole(1, b), whole(1, n), whole(b, n), whole(b, m), pl.BlockSpec((rows, m), lambda i: (i, 0))],
+        in_specs=[
+            whole(b, b), whole(1, b), whole(1, b), whole(1, n), whole(b, n), whole(*pc.shape), pl.BlockSpec((rows, m), lambda i: (i, 0)),
+        ],
         out_specs=[pl.BlockSpec((rows, m), lambda i: (i, 0)), whole(1, n)],
         out_shape=[jax.ShapeDtypeStruct((n, m), jnp.float32), jax.ShapeDtypeStruct((1, n), jnp.float32)],
-        scratch_shapes=[pltpu.VMEM((steps, 3 * b, rows), jnp.bfloat16), pltpu.VMEM((3 * b, m), jnp.bfloat16)],
+        scratch_shapes=[pltpu.VMEM((n, 3 * b), jnp.bfloat16), pltpu.VMEM((3 * b, m), jnp.bfloat16)],
     )(g, pred, rew, mean, pr, pc, cov)
-from jax.sharding import PartitionSpec as P
-
-MESH = pl.DeviceIdType.MESH
 
 
 def far_first(t, n):
@@ -92,10 +181,10 @@
     ctx_hbm, w_hbm, bias_hbm, cov_hbm, mean_hbm,
     g_out, pred_out, pr_out, pc_out,
     ctx_all, ctx_m, w_v, bias_v, cov_v, mean_v, c_hi, c_mid, c_lo,
-    x_send, x_recv, z_send, z_recv, phi_s, phi_c, phi_p, phi_r,
-    pp_send, pp_recv, p_own, g_send, g_recv, gz_s, gz_r, pz_s, pz_r, g_s, g_all,
+    x_send, x_recv, z_send, z_code, z_recv, phi_s, phi_c, phi_r,
+    pp_send, pp_recv, p_own, p_code, g_send, g_recv, gz_s, gz_r, pz_s, pz_r, g_s, g_all,
     pr_all, p_z, pc_all,
-    local, near, pair_s, pair_r, send, recv, mate,
+    local, near, pair_s, pair_r, send, recv, mate, send_pc, recv_pc,
 ):
     nz, nc, nb = z_send.shape[0], ctx_all.shape[0], 4
     r, c = lax.axis_index("row"), lax.axis_index("col")
@@ -192,7 +281,9 @@
         z_send[k] = own[a, b]
     swap_x.wait_recv()
     for k, (a, b) in enumerate(z_pieces):
-        z_send[k] += x_recv[a, b]
+        both = z_send[k] + x_recv[a, b]
+        z_send[k] = both
+        z_code[k] = coded_sum(both)
     pl.semaphore_wait(near, 2)
 
     def line_copy(src, dst, phase, t):
@@ -203,19 +294,19 @@
 
     def start_z(t, _):
         t = far_first(t, nz)
-        line_copy(z_send.at[(z + t) % nz], z_recv.at[z], 1, t).start()
+        line_copy(z_code.at[(z + t) % nz], z_recv.at[z], 1, t).start()
         return 0
 
     lax.fori_loop(0, nz - 1, start_z, 0)
-    z_recv[z] = z_send[z]
-
-    def wait_z(t, _):
-        line_arrival(z_recv, 1, (z + t) % nz).wait_recv()
-        return 0
-
-    lax.fori_loop(1, nz, wait_z, 0)
+
+    def add_z(t, acc):
+        zz = (z + near_first(t, nz)) % nz
+        line_arrival(z_recv, 1, zz).wait_recv()
+        return acc + sum_from(z_recv[zz])
+
+    total = lax.fori_loop(0, nz - 1, add_z, z_send[z])
     kb = z % 4
-    total = jnp.sum(z_recv[...], axis=0) + bias_v[:, pl.ds(pl.multiple_of(kb * 256, 256), 256)]
+    total = total + bias_v[:, pl.ds(pl.multiple_of(kb * 256, 256), 256)]
     phi = jnp.tanh(total).astype(jnp.bfloat16)
     phi_s[...] = phi
 
@@ -229,58 +320,42 @@
     def mate_copy(k):
         return remote(phi_c.at[h * nz + k], phi_c.at[h * nz + k], mate.at[0, k], mate.at[1, k], at(z, other, c))
 
+    def plane_copy(src, dst, phase, t):
+        return remote(src, dst, send.at[phase, t], recv.at[phase, c], at(z, h, (c + t) % nc))
+
+    holder = c == z
+
+    def push(core, k):
+        column = k % 4
+        slot = core * 8 + k // 4 * 2 + column % 2
+
+        @pl.when(jnp.logical_and(holder, column // 2 == h))
+        def _():
+            phi_r[slot] = phi_c[core * nz + k]
+
+            @pl.when(slot != z)
+            def _():
+                remote(phi_c.at[core * nz + k], phi_r.at[slot], send.at[3, slot], recv.at[4, slot], at(z, h, slot)).start()
+
     phi_c[h * nz + z] = phi
     mate_copy(z).start()
-
-    def plane_copy(src, dst, phase, t):
-        return remote(src, dst, send.at[phase, t], recv.at[phase, c], at(z, h, (c + t) % nc))
-
-    def start_plane_phi(t, _):
-        plane_copy(phi_s, phi_p.at[c], 3, t).start()
-        return 0
-
-    lax.fori_loop(1, nc, start_plane_phi, 0)
-    phi_p[c] = phi
-
-    goal = kb // 2
-    slot = h * 8 + z // 4 * 2 + kb % 2
-
-    def row_copy(t):
-        zz = (c + t) % nc
-        return remote(phi_p.at[zz], phi_r.at[slot], send.at[4, t], recv.at[4, slot], at(zz, goal, c))
-
-    def pass_phi(t, _):
-        zz = (c + t) % nc
-
-        @pl.when(t > 0)
-        def _():
-            plane_arrival(phi_p, 3, zz).wait_recv()
-
-        here = jnp.logical_and(zz == z, goal == h)
-
-        @pl.when(here)
-        def _():
-            phi_r[slot] = phi_p[zz]
-
-        @pl.when(jnp.logical_not(here))
-        def _():
-            row_copy(t).start()
-
-        return 0
-
-    lax.fori_loop(0, nc, pass_phi, 0)
+    push(h, z)
 
     def pass_mate(t, _):
         zz = (z + near_first(t, nz)) % nz
         remote(phi_s, phi_c.at[h * nz + zz], send.at[2, 0], recv.at[2, zz], at(z, other, c)).wait_recv()
         mate_copy(zz).start()
+        push(h, zz)
         return 0
 
     lax.fori_loop(0, nz - 1, pass_mate, 0)
 
     def wait_mate(t, _):
-        k = other * nz + t
-        remote(phi_c.at[k], phi_c.at[k], mate.at[0, t], mate.at[1, t], at(z, other, c)).wait_recv()
+        k = (z + near_first(t - 1, nz)) % nz
+        k = jnp.where(t == 0, z, k)
+        i = other * nz + k
+        remote(phi_c.at[i], phi_c.at[i], mate.at[0, k], mate.at[1, k], at(z, other, c)).wait_recv()
+        push(other, k)
         return 0
 
     lax.fori_loop(0, nz, wait_mate, 0)
@@ -302,21 +377,28 @@
     lax.fori_loop(1, nc, start_pp, 0)
     pp_recv[c] = pp_send[c]
 
-    def source_here(s):
-        zz = s % 8 // 2 * 4 + goal_of(s)
-        return jnp.logical_and(zz == z, s // 8 == h)
-
-    def goal_of(s):
-        return 2 * h + s % 2
-
-    def wait_row(s, _):
-        @pl.when(jnp.logical_not(source_here(s)))
-        def _():
-            plane_arrival(phi_r, 4, s).wait_recv()
-
-        return 0
-
-    lax.fori_loop(0, nz, wait_row, 0)
+    def pass_row(t):
+        return plane_copy(phi_r.at[c], phi_r.at[c], 4, t)
+
+    @pl.when(jnp.logical_not(holder))
+    def _():
+        plane_arrival(phi_r, 4, c).wait_recv()
+
+    def start_row(t, _):
+        @pl.when((c + t) % nc != z)
+        def _():
+            pass_row(t).start()
+
+        return 0
+
+    lax.fori_loop(1, nc, start_row, 0)
+
+    def wait_row(t, _):
+        @pl.when(jnp.logical_not(holder))
+        def _():
+            plane_arrival(phi_r, 4, (c + t) % nc).wait_recv()
+
+        return 0
 
     def wait_pp(t, _):
         plane_arrival(pp_recv, 5, (c + t) % nc).wait_recv()
@@ -325,14 +407,8 @@
     lax.fori_loop(1, nc, wait_pp, 0)
     p_mine = jnp.sum(pp_recv[...], axis=0)
     p_own[...] = p_mine
-
-    def start_pr(t, _):
-        plane_copy(p_own, pr_all.at[c], 6, t).start()
-        return 0
-
-    lax.fori_loop(1, nc, start_pr, 0)
-    pr_all[c] = p_mine
-    p_z[z] = p_mine
+    p_code[0] = coded_panel(p_mine)
+    lax.fori_loop(1, nc, wait_row, 0)
 
     width = p_mine.shape[1]
     zeros = jnp.zeros((7, width), jnp.float32)
@@ -348,6 +424,15 @@
     g_send[...] = gram[:16] + gram[16:32] + gram[32:]
     swap_g = remote(g_send, g_recv, pair_s.at[1], pair_r.at[1], at(z, other, c))
     swap_g.start()
+
+    def start_pr(t, _):
+        plane_copy(p_own, pr_all.at[c], 6, t).start()
+        return 0
+
+    lax.fori_loop(1, nc, start_pr, 0)
+    pr_all[c] = p_mine
+    p_z[z] = p_code[0]
+
     swap_g.wait_recv()
     both = g_send[...] + g_recv[...]
     gz_s[...] = both[:8]
@@ -365,7 +450,7 @@
 
     def start_pz(t, _):
         t = far_first(t, nz)
-        line_copy(p_own, p_z.at[z], 9, t).start()
+        line_copy(p_code.at[0], p_z.at[z], 9, t).start()
         return 0
 
     lax.fori_loop(0, nz - 1, start_pz, 0)
@@ -388,11 +473,12 @@
     g_all[c] = g_rows
     pred_out[...] = jnp.sum(pz_r[...], axis=0)
 
-    def col_copy(zz):
-        return remote(p_z.at[zz], pc_all.at[h, c], send.at[11, zz], recv.at[11, c], at(z, h, zz))
+    def col_copy(zz, core):
+        return remote(p_z.at[zz], pc_all.at[h, c], send_pc.at[core, zz], recv_pc.at[h, c], at(z, core, zz))
 
     def pass_pz(t, _):
-        zz = (z + t) % nz
+        zz = (z + near_first(t - 1, nz)) % nz
+        zz = jnp.where(t == 0, z, zz)
 
         @pl.when(t > 0)
         def _():
@@ -404,26 +490,12 @@
 
         @pl.when(zz != c)
         def _():
-            col_copy(zz).start()
-
+            col_copy(zz, h).start()
+
+        col_copy(zz, other).start()
         return 0
 
     lax.fori_loop(0, nz, pass_pz, 0)
-
-    def mate_pc(p):
-        return remote(pc_all.at[h, p], pc_all.at[h, p], mate.at[2, p], mate.at[3, p], at(z, other, c))
-
-    def pass_pc(t, _):
-        p = (c + t) % nc
-
-        @pl.when(t > 0)
-        def _():
-            remote(p_own, pc_all.at[h, p], send.at[11, 0], recv.at[11, p], at(z, other, c)).wait_recv()
-
-        mate_pc(p).start()
-        return 0
-
-    lax.fori_loop(0, nc, pass_pc, 0)
 
     def wait_last(t, _):
         p = (c + t) % nc
@@ -435,27 +507,36 @@
     g_out[...] = g_all[...].reshape(g_out.shape)
     pr_out[...] = pr_all[...].reshape(pr_out.shape)
 
-    def wait_pc(p, _):
-        remote(p_own, pc_all.at[other, p], mate.at[2, p], mate.at[3, p], at(z, other, c)).wait_recv()
+    def wait_pc(t, _):
+        p = (c + t) % nc
+
+        @pl.when(t > 0)
+        def _():
+            remote(p_code.at[0], pc_all.at[h, p], send_pc.at[0, 0], recv_pc.at[h, p], at(z, other, c)).wait_recv()
+
+        remote(p_code.at[0], pc_all.at[other, p], send_pc.at[0, 0], recv_pc.at[other, p], at(z, other, c)).wait_recv()
         return 0
 
     lax.fori_loop(0, nc, wait_pc, 0)
-    for k in range(2):
-        pc_out[:, k * width : (k + 1) * width] = pc_all[k].reshape(tokens, width)
+    pc_out[...] = pc_all[...]
 
     swap_x.wait_send()
     swap_g.wait_send()
 
     def sent(t, _):
         ctx_copy(t).wait_send()
-        line_copy(z_send.at[(z + t) % nz], z_recv.at[z], 1, t).wait_send()
+        line_copy(z_code.at[(z + t) % nz], z_recv.at[z], 1, t).wait_send()
         line_copy(phi_s, phi_c.at[h * nz + z], 2, t).wait_send()
-        plane_copy(phi_s, phi_p.at[c], 3, t).wait_send()
+
+        @pl.when((c + t) % nc != z)
+        def _():
+            pass_row(t).wait_send()
+
         plane_copy(pp_send.at[(c + t) % nc], pp_recv.at[c], 5, t).wait_send()
         plane_copy(p_own, pr_all.at[c], 6, t).wait_send()
         line_copy(gz_s, gz_r.at[z], 7, t).wait_send()
         line_copy(pz_s, pz_r.at[z], 8, t).wait_send()
-        line_copy(p_own, p_z.at[z], 9, t).wait_send()
+        line_copy(p_code.at[0], p_z.at[z], 9, t).wait_send()
         plane_copy(g_s, g_all.at[c], 10, t).wait_send()
         return 0
 
@@ -463,15 +544,15 @@
 
     def sent_some(t, _):
         mate_copy(t).wait_send()
-        mate_pc(t).wait_send()
-
-        @pl.when(jnp.logical_not(jnp.logical_and((c + t) % nc == z, goal == h)))
-        def _():
-            row_copy(t).wait_send()
+        col_copy(t, other).wait_send()
 
         @pl.when(t != c)
         def _():
-            col_copy(t).wait_send()
+            col_copy(t, h).wait_send()
+
+        @pl.when(jnp.logical_and(holder, t != z))
+        def _():
+            remote(phi_r.at[t], phi_r.at[t], send.at[3, t], recv.at[4, t], at(z, h, t)).wait_send()
 
         return 0
 
@@ -488,18 +569,18 @@
     scratch = [
         vmem((nc, rows_here, depth), bf16), vmem((b, depth), bf16), vmem((depth, m), bf16), vmem((1, m), f32),
         vmem((n, m), f32), vmem((1, n), f32), vmem((n, m), bf16), vmem((n, m), bf16), vmem((n, m), bf16),
-        vmem((b // 2, m), f32), vmem((b // 2, m), f32), vmem((nz, 16, 256), f32), vmem((nz, 16, 256), f32),
-        vmem((16, 256), bf16), vmem((2 * nz, 16, 256), bf16), vmem((nc, 16, 256), bf16), vmem((16, 16, 256), bf16),
-        vmem((nc, 8, n), f32), vmem((nc, 8, n), f32), vmem((8, n), f32), vmem((16, b), f32), vmem((16, b), f32),
+        vmem((b // 2, m), f32), vmem((b // 2, m), f32), vmem((nz, 16, 256), f32), vmem((nz, 16, 256), bf16), vmem((nz, 16, 256), bf16),
+        vmem((16, 256), bf16), vmem((2 * nz, 16, 256), bf16), vmem((16, 16, 256), bf16),
+        vmem((nc, 8, n), f32), vmem((nc, 8, n), f32), vmem((8, n), f32), vmem((1, 8, n), bf16), vmem((16, b), f32), vmem((16, b), f32),
         vmem((8, b), f32), vmem((nz, 8, b), f32), vmem((1, b), f32), vmem((nz, 1, b), f32), vmem((8, b), f32), vmem((nc, 8, b), f32),
-        vmem((nc, 8, n), f32), vmem((nz, 8, n), f32), vmem((2, nc, 8, n), f32),
-        sem.DMA((5,)), sem.REGULAR, sem.DMA((2,)), sem.DMA((2,)), sem.DMA((12, 16)), sem.DMA((12, 16)), sem.DMA((4, 16)),
+        vmem((nc, 8, n), f32), vmem((nz, 8, n), bf16), vmem((2, nc, 8, n), bf16),
+        sem.DMA((5,)), sem.REGULAR, sem.DMA((2,)), sem.DMA((2,)), sem.DMA((11, 16)), sem.DMA((11, 16)), sem.DMA((2, 16)), sem.DMA((2, 16)), sem.DMA((2, 16)),
     ]
     return pl.pallas_call(
         exchange_kernel,
         in_specs=[pl.BlockSpec(memory_space=pl.ANY)] * 5,
         out_specs=[pl.BlockSpec(memory_space=pltpu.VMEM)] * 4,
-        out_shape=[jax.ShapeDtypeStruct(s, f32) for s in ((b, b), (1, b), (b, n), (b, m))],
+        out_shape=[jax.ShapeDtypeStruct(s, f32) for s in ((b, b), (1, b), (b, n))] + [jax.ShapeDtypeStruct((2, nc, 8, n), bf16)],
         scratch_shapes=scratch,
         compiler_params=pltpu.CompilerParams(collective_id=0, has_side_effects=True),
     )(context, weight, bias, covariance, mean)

time: 100 us -> 82.7 us (0.83)
  the two profiles are of different devices: /device:TPU:33 before, /device:TPU:1 now
where the time goes in v2:
time: 82.7 us; the launch traced here: 81.8 us
  Pallas kernels  81.2 us (98%)
    pallas_call x1, Pallas kernels, exchange(): pl.pallas_call(exchange_kernel, in_specs=[pl.BlockSpec(memory_space=pl.AN...  69.6 us
    pallas_call x1, Pallas kernels, update(): pl.pallas_call(update_kernel, grid=(steps,), in_specs=[whole(b, b), whole...  11.6 us

profile of v2, /device:TPU:1, one launch (start us, length us, event | category | flops | bytes accessed | tf_op | source)
XLA Modules:
  0.0 81.8 jit_solution(3673348768534821593)
XLA Ops:
  0.6 69.6 %shard_map.77 = (f32[128,128]{1,0:T(8,128)}, f32[1,128]{1,0:T(1,128)}, f32[128,512]{1,0:T(8,128)}, bf16[2,16,8,512]{3,2,1,0:T(8,128)(2,1)}) custom-call(bf16[8,256]{1,0:T(8,128)(2,1)} %ctx_hbm.1, bf16[256,1024]{1,0:T(8,128)(2,1)} %w_hbm.1, f32[1,1024]{1,0:T(1,128)} %bitcast.6, f32[512,1024]{1,0:T(8,128)} %cov_ref.1, f32[1,512]{1,0:T(1,128)} %bitcast.4), custom_call_target="tpu_custom_call" | custom-call | tf_op jit(solution)/shard_map/pallas_call | solution.py:579
  70.2 11.6 %shard_map.78 = (f32[512,1024]{1,0:T(8,128)}, f32[1,512]{1,0:T(1,128)}) custom-call(f32[128,128]{1,0:T(8,128)} %get-tuple-element.8.g_ref, f32[1,128]{1,0:T(1,128)} %get-tuple-element.9.pred_ref, f32[1,128]{1,0:T(1,128)} %bitcast.7, f32[1,512]{1,0:T(1,128)} %bitcast.5, f32[128,512]{1,0:T(8,128)} %get-tuple-element.10.pr_ref, ...), custom_call_target="tpu_custom_call" | custom-call | tf_op jit(solution)/shard_map/pallas_call | solution.py:160

commit v3 on v2

--- a/solution.py
+++ b/solution.py
@@ -103,70 +103,40 @@
     return jnp.dot(jnp.concatenate([ah, ah, am, am, ah, al], 1), jnp.concatenate([bh, bm, bh, bm, bl, bh], 0), preferred_element_type=jnp.float32)
 
 
-def spd_inverse(a, w):
-    n = a.shape[0]
+def eliminated(blocks, lo, w):
+    n = blocks[0].shape[1]
     lane = lax.broadcasted_iota(jnp.int32, (8, n), 1)
     sub = lax.broadcasted_iota(jnp.int32, (8, n), 0)
-    blocks = [a[8 * i : 8 * i + 8] for i in range(n // 8)]
-    for lo in range(0, n, w):
-        first, last = lo // 8, (lo + w) // 8
-        panel = panel4(blocks[first:last], lo, lane, sub)
-        rest = blocks[:first] + blocks[last:]
-        cols = jnp.concatenate([b[:, lo : lo + w] for b in rest], 0)
-        prod = dot3(cols, jnp.concatenate(panel, 0))
-        inside = (lane >= lo) & (lane < lo + w)
-        rest = [jnp.where(inside, 0.0, b) - prod[8 * i : 8 * i + 8] for i, b in enumerate(rest)]
-        blocks = rest[:first] + panel + rest[first:]
-    return jnp.concatenate(blocks, 0)
-
-
-def update_kernel(g_ref, pred_ref, rew_ref, mean_ref, pr_ref, pc_ref, cov_ref, out_ref, outm_ref, gain_s, pc_s):
-    step = pl.program_id(0)
-    rows = cov_ref.shape[0]
-
-    @pl.when(step == 0)
+    first, last = lo // 8, (lo + w) // 8
+    panel = panel4(blocks[first:last], lo, lane, sub)
+    rest = blocks[:first] + blocks[last:]
+    cols = jnp.concatenate([b[:, lo : lo + w] for b in rest], 0)
+    prod = dot3(cols, jnp.concatenate(panel, 0))
+    inside = (lane >= lo) & (lane < lo + w)
+    rest = [jnp.where(inside, 0.0, b) - prod[8 * i : 8 * i + 8] for i, b in enumerate(rest)]
+    return rest[:first] + panel + rest[first:]
+
+
+def update_kernel(gain_ref, pc_ref, shift_ref, mean_ref, cov_ref, out_ref, outm_ref):
+    out_ref[...] = cov_ref[...] - jnp.dot(gain_ref[...], pc_ref[...], preferred_element_type=jnp.float32)
+
+    @pl.when(pl.program_id(0) == 0)
     def _():
-        b = g_ref.shape[0]
-        width = pc_ref.shape[-1]
-        for k in range(2):
-            panel = panel_from(pc_ref[k]).reshape(b, width)
-            hi, mid, _ = split3(panel)
-            cut = slice(k * width, k * width + width)
-            pc_s[:b, cut] = hi
-            pc_s[b : 2 * b, cut] = mid
-            pc_s[2 * b :, cut] = hi
-        pr = pr_ref[...]
-        pr_t = pr.T
-        eye = (lax.broadcasted_iota(jnp.int32, (b, b), 0) == lax.broadcasted_iota(jnp.int32, (b, b), 1)).astype(jnp.float32)
-        inv = spd_inverse(g_ref[...] + eye, 16)
-        gain = jnp.dot(pr_t, inv, precision=HI, preferred_element_type=jnp.float32)
-        hi, mid, _ = split3(gain)
-        gain_s[:, :b] = hi
-        gain_s[:, b : 2 * b] = hi
-        gain_s[:, 2 * b :] = mid
-        diff = rew_ref[...] - pred_ref[...]
-        coeffs = jnp.dot(jnp.broadcast_to(diff, (8, b)), inv, precision=HI, preferred_element_type=jnp.float32)
-        outm_ref[...] = mean_ref[...] + jnp.dot(coeffs, pr, precision=HI, preferred_element_type=jnp.float32)[:1]
-
-    mine = gain_s[pl.ds(pl.multiple_of(step * rows, rows), rows), :]
-    out_ref[...] = cov_ref[...] - jnp.dot(mine, pc_s[...], preferred_element_type=jnp.float32)
-
-
-def update(g, pred, rew, mean, pr, pc, cov, steps=4):
-    b = g.shape[0]
+        outm_ref[...] = mean_ref[...] + shift_ref[...]
+
+
+def update(gain, panel, shift, mean, cov, steps=4):
     n, m = cov.shape
     rows = n // steps
     whole = lambda *shape: pl.BlockSpec(shape, lambda i: (0,) * len(shape))
+    cut = lambda width: pl.BlockSpec((rows, width), lambda i: (i, 0))
     return pl.pallas_call(
         update_kernel,
         grid=(steps,),
-        in_specs=[
-            whole(b, b), whole(1, b), whole(1, b), whole(1, n), whole(b, n), whole(*pc.shape), pl.BlockSpec((rows, m), lambda i: (i, 0)),
-        ],
-        out_specs=[pl.BlockSpec((rows, m), lambda i: (i, 0)), whole(1, n)],
+        in_specs=[cut(gain.shape[1]), whole(*panel.shape), whole(1, n), whole(1, n), cut(m)],
+        out_specs=[cut(m), whole(1, n)],
         out_shape=[jax.ShapeDtypeStruct((n, m), jnp.float32), jax.ShapeDtypeStruct((1, n), jnp.float32)],
-        scratch_shapes=[pltpu.VMEM((n, 3 * b), jnp.bfloat16), pltpu.VMEM((3 * b, m), jnp.bfloat16)],
-    )(g, pred, rew, mean, pr, pc, cov)
+    )(gain, panel, shift, mean, cov)
 
 
 def far_first(t, n):
@@ -178,15 +148,15 @@
 
 
 def exchange_kernel(
-    ctx_hbm, w_hbm, bias_hbm, cov_hbm, mean_hbm,
-    g_out, pred_out, pr_out, pc_out,
-    ctx_all, ctx_m, w_v, bias_v, cov_v, mean_v, c_hi, c_mid, c_lo,
+    ctx_hbm, w_hbm, bias_hbm, cov_hbm, mean_hbm, rew_hbm,
+    gain_out, pc_out, shift_out,
+    ctx_all, ctx_m, w_v, bias_v, cov_v, mean_v, rew_v, c_hi, c_mid,
     x_send, x_recv, z_send, z_code, z_recv, phi_s, phi_c, phi_r,
-    pp_send, pp_recv, p_own, p_code, g_send, g_recv, gz_s, gz_r, pz_s, pz_r, g_s, g_all,
+    pp_send, pp_recv, p_own, p_code, gz_s, gz_r, pz_s, pz_r, g_s, g_all, pred_s, pred_r,
     pr_all, p_z, pc_all,
-    local, near, pair_s, pair_r, send, recv, mate, send_pc, recv_pc,
+    local, near, pair_s, pair_r, send, recv, mate, send_pc, recv_pc, send_g, recv_g,
 ):
-    nz, nc, nb = z_send.shape[0], ctx_all.shape[0], 4
+    nz, nc, nb = z_recv.shape[0], ctx_all.shape[0], 4
     r, c = lax.axis_index("row"), lax.axis_index("col")
     z, h = r // 2, r % 2
     other = 1 - h
@@ -205,6 +175,7 @@
         pltpu.make_async_copy(w_hbm, w_v, local.at[2]),
         pltpu.make_async_copy(bias_hbm, bias_v, local.at[3]),
         pltpu.make_async_copy(mean_hbm, mean_v, local.at[4]),
+        pltpu.make_async_copy(rew_hbm, rew_v, local.at[5]),
     ]
     for load in loads:
         load.start()
@@ -246,20 +217,13 @@
 
     loads[1].wait()
     rows = cov_v.shape[0]
-
-    def split_cov(i, _):
-        cut = pl.ds(pl.multiple_of(i * 64, 64), 64)
-        hi, mid, lo = split3(cov_v[cut, :])
-        c_hi[cut, :] = hi
-        c_mid[cut, :] = mid
-        c_lo[cut, :] = lo
-        return 0
-
-    lax.fori_loop(0, rows // 64, split_cov, 0)
-    loads[2].wait()
-    loads[3].wait()
-    loads[4].wait()
-    loads[0].wait()
+    for i in range(rows // 128):
+        cut = slice(i * 128, i * 128 + 128)
+        hi, mid, _ = split3(cov_v[cut, :].T)
+        c_hi[:, cut] = hi
+        c_mid[:, cut] = mid
+    for load in loads[:1] + loads[2:]:
+        load.wait()
 
     def wait_ctx(t, _):
         plane_arrival(ctx_all, 0, (c + t) % nc).wait_recv()
@@ -271,20 +235,7 @@
     ctx_m[...] = ctx_all[...].astype(jnp.float32).reshape(tokens, depth).astype(jnp.bfloat16)
 
     theirs = ctx_m[pl.ds(pl.multiple_of(other * half, half), half), :]
-    x_send[...] = jnp.dot(theirs, w_v[...], preferred_element_type=jnp.float32)
-    swap_x = remote(x_send, x_recv, pair_s.at[0], pair_r.at[0], at(z, other, c))
-    swap_x.start()
     mine = ctx_m[pl.ds(pl.multiple_of(h * half, half), half), :]
-    own = jnp.dot(mine, w_v[...], preferred_element_type=jnp.float32)
-    z_pieces = [(slice(k // 4 * 16, k // 4 * 16 + 16), slice(k % 4 * 256, k % 4 * 256 + 256)) for k in range(nz)]
-    for k, (a, b) in enumerate(z_pieces):
-        z_send[k] = own[a, b]
-    swap_x.wait_recv()
-    for k, (a, b) in enumerate(z_pieces):
-        both = z_send[k] + x_recv[a, b]
-        z_send[k] = both
-        z_code[k] = coded_sum(both)
-    pl.semaphore_wait(near, 2)
 
     def line_copy(src, dst, phase, t):
         return remote(src, dst, send.at[phase, t], recv.at[phase, z], at((z + t) % nz, h, c))
@@ -292,20 +243,47 @@
     def line_arrival(buf, phase, src):
         return remote(buf.at[src], buf.at[src], send.at[phase, 0], recv.at[phase, src], at(z, other, c))
 
-    def start_z(t, _):
-        t = far_first(t, nz)
-        line_copy(z_code.at[(z + t) % nz], z_recv.at[z], 1, t).start()
-        return 0
-
-    lax.fori_loop(0, nz - 1, start_z, 0)
+    def columns(block):
+        return w_v[:, pl.ds(pl.multiple_of(block * 256, 256), 256)]
+
+    def swap_x(block):
+        return remote(x_send.at[block], x_recv.at[block], pair_s.at[block], pair_r.at[block], at(z, other, c))
+
+    order = [(z + t) % 4 for t in (0, 1, 3, 2)]
+    for block in order:
+        x_send[block] = jnp.dot(theirs, columns(block), preferred_element_type=jnp.float32)
+        swap_x(block).start()
+    for t, block in zip((0, 1, 3, 2), order):
+        z_send[block] = jnp.dot(mine, columns(block), preferred_element_type=jnp.float32)
+    pl.semaphore_wait(near, 2)
+    for t, block in zip((0, 1, 3, 2), order):
+        swap_x(block).wait_recv()
+        both = z_send[block] + x_recv[block]
+        z_send[block] = both
+        z_code[block] = coded_sum(both).reshape(4, 16, 256)
+
+        def start_z(i, _):
+            step = t + (i * 4 + 8) % nz
+            row = (z + step) % nz // 4
+
+            @pl.when(step > 0)
+            def _():
+                remote(
+                    z_code.at[block, row], z_recv.at[z], send.at[1, step], recv.at[1, z], at((z + step) % nz, h, c)
+                ).start()
+
+            return 0
+
+        lax.fori_loop(0, 4, start_z, 0)
 
     def add_z(t, acc):
         zz = (z + near_first(t, nz)) % nz
         line_arrival(z_recv, 1, zz).wait_recv()
         return acc + sum_from(z_recv[zz])
 
-    total = lax.fori_loop(0, nz - 1, add_z, z_send[z])
     kb = z % 4
+    own = z_send[kb, pl.ds(pl.multiple_of(z // 4 * 16, 16), 16), :]
+    total = lax.fori_loop(0, nz - 1, add_z, own)
     total = total + bias_v[:, pl.ds(pl.multiple_of(kb * 256, 256), 256)]
     phi = jnp.tanh(total).astype(jnp.bfloat16)
     phi_s[...] = phi
@@ -363,10 +341,8 @@
     part = None
     for k in range(4):
         lhs = jnp.concatenate([phi_c[i * 4 + k] for i in range(8)], 0)
-        for term in (c_hi, c_mid, c_lo):
-            prod = lax.dot_general(
-                lhs, term[:, k * 256 : k * 256 + 256], (((1,), (1,)), ((), ())), preferred_element_type=jnp.float32
-            )
+        for term in (c_hi, c_mid):
+            prod = jnp.dot(lhs, term[k * 256 : k * 256 + 256, :], preferred_element_type=jnp.float32)
             part = prod if part is None else part + prod
     pp_send[...] = part.reshape(pp_send.shape)
 
@@ -421,22 +397,10 @@
             stacked[:, k * 256 : k * 256 + 256], rhs, (((1,), (1,)), ((), ())), preferred_element_type=jnp.float32
         )
         gram = prod if gram is None else gram + prod
-    g_send[...] = gram[:16] + gram[16:32] + gram[32:]
-    swap_g = remote(g_send, g_recv, pair_s.at[1], pair_r.at[1], at(z, other, c))
-    swap_g.start()
-
-    def start_pr(t, _):
-        plane_copy(p_own, pr_all.at[c], 6, t).start()
-        return 0
-
-    lax.fori_loop(1, nc, start_pr, 0)
-    pr_all[c] = p_mine
-    p_z[z] = p_code[0]
-
-    swap_g.wait_recv()
-    both = g_send[...] + g_recv[...]
+    both = gram[:16] + gram[16:32] + gram[32:]
     gz_s[...] = both[:8]
     pz_s[...] = both[8:9]
+    p_z[z] = p_code[0]
 
     def start_gz(t, _):
         t = far_first(t, nz)
@@ -462,16 +426,51 @@
         return 0
 
     lax.fori_loop(1, nz, wait_gz, 0)
-    g_rows = jnp.sum(gz_r[...], axis=0)
-    g_s[...] = g_rows
+    g_s[...] = jnp.sum(gz_r[...], axis=0)
+    pred_s[...] = jnp.sum(pz_r[...], axis=0)
+    swap_pred = remote(pred_s, pred_r, pair_s.at[4], pair_r.at[4], at(z, other, c))
+    swap_pred.start()
+
+    def g_copy(t, core):
+        return remote(g_s, g_all.at[h, c], send_g.at[core, t], recv_g.at[h, c], at(z, core, (c + t) % nc))
+
+    def g_arrival(core, p):
+        return remote(g_s, g_all.at[core, p], send_g.at[0, 0], recv_g.at[core, p], at(z, other, c))
 
     def start_g(t, _):
-        plane_copy(g_s, g_all.at[c], 10, t).start()
-        return 0
-
-    lax.fori_loop(1, nc, start_g, 0)
-    g_all[c] = g_rows
-    pred_out[...] = jnp.sum(pz_r[...], axis=0)
+        @pl.when(t > 0)
+        def _():
+            g_copy(t, h).start()
+
+        g_copy(t, other).start()
+        return 0
+
+    lax.fori_loop(0, nc, start_g, 0)
+    g_all[h, c] = g_s[...]
+
+    def start_pr(t, _):
+        plane_copy(p_own, pr_all.at[c], 6, t).start()
+        return 0
+
+    lax.fori_loop(1, nc, start_pr, 0)
+    pr_all[c] = p_own[...]
+
+    def wait_g(t, _):
+        p = (c + t) % nc
+
+        @pl.when(t > 0)
+        def _():
+            g_arrival(h, p).wait_recv()
+
+        g_arrival(other, p).wait_recv()
+        return 0
+
+    lax.fori_loop(0, nc, wait_g, 0)
+    eye = (lax.broadcasted_iota(jnp.int32, (tokens, tokens), 0) == lax.broadcasted_iota(jnp.int32, (tokens, tokens), 1)).astype(jnp.float32)
+    g = (g_all[0] + g_all[1]).reshape(tokens, tokens) + eye
+    blocks = [g[8 * i : 8 * i + 8] for i in range(tokens // 8)]
+    for lo in range(0, 48, 16):
+        blocks = eliminated(blocks, lo, 16)
 
     def col_copy(zz, core):
         return remote(p_z.at[zz], pc_all.at[h, c], send_pc.at[core, zz], recv_pc.at[h, c], at(z, core, zz))
@@ -497,15 +496,15 @@
 
     lax.fori_loop(0, nz, pass_pz, 0)
 
+    for lo in range(48, 96, 16):
+        blocks = eliminated(blocks, lo, 16)
+
     def wait_last(t, _):
         p = (c + t) % nc
         plane_arrival(pr_all, 6, p).wait_recv()
-        plane_arrival(g_all, 10, p).wait_recv()
         return 0
 
     lax.fori_loop(1, nc, wait_last, 0)
-    g_out[...] = g_all[...].reshape(g_out.shape)
-    pr_out[...] = pr_all[...].reshape(pr_out.shape)
 
     def wait_pc(t, _):
         p = (c + t) % nc
@@ -518,14 +517,35 @@
         return 0
 
     lax.fori_loop(0, nc, wait_pc, 0)
-    pc_out[...] = pc_all[...]
-
-    swap_x.wait_send()
-    swap_g.wait_send()
+    swap_pred.wait()
+
+    for k in range(2):
+        panel = panel_from(pc_all[k]).reshape(tokens, width)
+        hi, mid, _ = split3(panel)
+        cut = slice(k * width, k * width + width)
+        pc_out[:tokens, cut] = hi
+        pc_out[tokens : 2 * tokens, cut] = mid
+        pc_out[2 * tokens :, cut] = hi
+    pr = pr_all[...].reshape(tokens, width)
+    pr_t = pr.T
+    for lo in range(96, 128, 16):
+        blocks = eliminated(blocks, lo, 16)
+    inv = jnp.concatenate(blocks, 0)
+    gain = jnp.dot(pr_t, inv, precision=HI, preferred_element_type=jnp.float32)
+    hi, mid, _ = split3(gain)
+    gain_out[:, :tokens] = hi
+    gain_out[:, tokens : 2 * tokens] = hi
+    gain_out[:, 2 * tokens :] = mid
+    diff = rew_v[...] - (pred_s[...] + pred_r[...])
+    coeffs = jnp.dot(jnp.broadcast_to(diff, (8, tokens)), inv, precision=HI, preferred_element_type=jnp.float32)
+    shift_out[...] = jnp.dot(coeffs, pr, precision=HI, preferred_element_type=jnp.float32)[:1]
+
+    for block in range(4):
+        swap_x(block).wait_send()
 
     def sent(t, _):
         ctx_copy(t).wait_send()
-        line_copy(z_code.at[(z + t) % nz], z_recv.at[z], 1, t).wait_send()
+        remote(phi_s, z_recv.at[z], send.at[1, t], recv.at[1, z], at((z + t) % nz, h, c)).wait_send()
         line_copy(phi_s, phi_c.at[h * nz + z], 2, t).wait_send()
 
         @pl.when((c + t) % nc != z)
@@ -537,7 +557,7 @@
         line_copy(gz_s, gz_r.at[z], 7, t).wait_send()
         line_copy(pz_s, pz_r.at[z], 8, t).wait_send()
         line_copy(p_code.at[0], p_z.at[z], 9, t).wait_send()
-        plane_copy(g_s, g_all.at[c], 10, t).wait_send()
+        g_copy(t, h).wait_send()
         return 0
 
     lax.fori_loop(1, nz, sent, 0)
@@ -545,6 +565,7 @@
     def sent_some(t, _):
         mate_copy(t).wait_send()
         col_copy(t, other).wait_send()
+        g_copy(t, other).wait_send()
 
         @pl.when(t != c)
         def _():
@@ -559,7 +580,7 @@
     lax.fori_loop(0, nz, sent_some, 0)
 
 
-def exchange(context, weight, bias, covariance, mean):
+def exchange(context, weight, bias, covariance, mean, rewards):
     rows_here, depth = context.shape
     n, m = covariance.shape
     nz, nc = lax.axis_size("row") // 2, lax.axis_size("col")
@@ -568,28 +589,33 @@
     vmem, sem = pltpu.VMEM, pltpu.SemaphoreType
     scratch = [
         vmem((nc, rows_here, depth), bf16), vmem((b, depth), bf16), vmem((depth, m), bf16), vmem((1, m), f32),
-        vmem((n, m), f32), vmem((1, n), f32), vmem((n, m), bf16), vmem((n, m), bf16), vmem((n, m), bf16),
-        vmem((b // 2, m), f32), vmem((b // 2, m), f32), vmem((nz, 16, 256), f32), vmem((nz, 16, 256), bf16), vmem((nz, 16, 256), bf16),
+        vmem((n, m), f32), vmem((1, n), f32), vmem((1, b), f32), vmem((m, n), bf16), vmem((m, n), bf16),
+        vmem((4, b // 2, 256), f32), vmem((4, b // 2, 256), f32), vmem((4, b // 2, 256), f32),
+        vmem((4, 4, 16, 256), bf16), vmem((nz, 16, 256), bf16),
         vmem((16, 256), bf16), vmem((2 * nz, 16, 256), bf16), vmem((16, 16, 256), bf16),
-        vmem((nc, 8, n), f32), vmem((nc, 8, n), f32), vmem((8, n), f32), vmem((1, 8, n), bf16), vmem((16, b), f32), vmem((16, b), f32),
-        vmem((8, b), f32), vmem((nz, 8, b), f32), vmem((1, b), f32), vmem((nz, 1, b), f32), vmem((8, b), f32), vmem((nc, 8, b), f32),
+        vmem((nc, 8, n), f32), vmem((nc, 8, n), f32), vmem((8, n), f32), vmem((1, 8, n), bf16),
+        vmem((8, b), f32), vmem((nz, 8, b), f32), vmem((1, b), f32), vmem((nz, 1, b), f32), vmem((8, b), f32), vmem((2, nc, 8, b), f32),
+        vmem((1, b), f32), vmem((1, b), f32),
         vmem((nc, 8, n), f32), vmem((nz, 8, n), bf16), vmem((2, nc, 8, n), bf16),
-        sem.DMA((5,)), sem.REGULAR, sem.DMA((2,)), sem.DMA((2,)), sem.DMA((11, 16)), sem.DMA((11, 16)), sem.DMA((2, 16)), sem.DMA((2, 16)), sem.DMA((2, 16)),
+        sem.DMA((6,)), sem.REGULAR, sem.DMA((5,)), sem.DMA((5,)), sem.DMA((10, 16)), sem.DMA((10, 16)), sem.DMA((2, 16)),
+        sem.DMA((2, 16)), sem.DMA((2, 16)), sem.DMA((2, 16)), sem.DMA((2, 16)),
     ]
     return pl.pallas_call(
         exchange_kernel,
-        in_specs=[pl.BlockSpec(memory_space=pl.ANY)] * 5,
-        out_specs=[pl.BlockSpec(memory_space=pltpu.VMEM)] * 4,
-        out_shape=[jax.ShapeDtypeStruct(s, f32) for s in ((b, b), (1, b), (b, n))] + [jax.ShapeDtypeStruct((2, nc, 8, n), bf16)],
+        in_specs=[pl.BlockSpec(memory_space=pl.ANY)] * 6,
+        out_specs=[pl.BlockSpec(memory_space=pltpu.VMEM)] * 3,
+        out_shape=[
+            jax.ShapeDtypeStruct((n, 3 * b), bf16), jax.ShapeDtypeStruct((3 * b, m), bf16), jax.ShapeDtypeStruct((1, n), f32),
+        ],
         scratch_shapes=scratch,
         compiler_params=pltpu.CompilerParams(collective_id=0, has_side_effects=True),
-    )(context, weight, bias, covariance, mean)
+    )(context, weight, bias, covariance, mean, rewards)
 
 
 def per_device(context, weight, feature_bias, covariance, prior_mean, rewards):
     mean = prior_mean.reshape(1, -1)
-    g, pred, pr, pc = exchange(context, weight, feature_bias.reshape(1, -1), covariance, mean)
-    cov, mean = update(g, pred, rewards.reshape(1, -1), mean, pr, pc, covariance)
+    gain, panel, shift = exchange(context, weight, feature_bias.reshape(1, -1), covariance, mean, rewards.reshape(1, -1))
+    cov, mean = update(gain, panel, shift, mean, covariance)
     return cov, mean.reshape(-1)
 
 

time: 82.7 us -> 86.3 us (1.044)
  Pallas kernels: 81.2 us -> 85.4 us
    pallas_call x1, Pallas kernels: 69.6 us -> 80.7 us  [exchange(): pl.pallas_call(exchange_kernel, in_specs=[pl.BlockSpec(memory_space=pl.AN...]
    pallas_call x1, Pallas kernels: 11.6 us -> 4.71 us  [update(): pl.pallas_call(update_kernel, grid=(steps,), in_specs=[cut(gain.shape[1])...]
where the time goes in v3:
time: 86.3 us; the launch traced here: 86.1 us
  Pallas kernels  85.4 us (99%)
    pallas_call x1, Pallas kernels, exchange(): pl.pallas_call(exchange_kernel, in_specs=[pl.BlockSpec(memory_space=pl.AN...  80.7 us
    pallas_call x1, Pallas kernels, update(): pl.pallas_call(update_kernel, grid=(steps,), in_specs=[cut(gain.shape[1])...  4.71 us

profile of v3, /device:TPU:1, one launch (start us, length us, event | category | flops | bytes accessed | tf_op | source)
XLA Modules:
  0.0 86.1 jit_solution(13320560872775186448)
XLA Ops:
  0.6 80.7 %shard_map.77 = (bf16[512,384]{1,0:T(8,128)(2,1)}, bf16[384,1024]{1,0:T(8,128)(2,1)}, f32[1,512]{1,0:T(1,128)}) custom-call(bf16[8,256]{1,0:T(8,128)(2,1)} %ctx_hbm.1, bf16[256,1024]{1,0:T(8,128)(2,1)} %w_hbm.1, f32[1,1024]{1,0:T(1,128)} %bitcast.6, f32[512,1024]{1,0:T(8,128)} %cov_ref.1, f32[1,512]{1,0:T(1,128)} %bitcast.4, f32[1,128]{1,0:T(1,128)} %bitcast.7), custom_call_target="tpu_custom_call" | custom-call | tf_op jit(solution)/shard_map/pallas_call | solution.py:603
  81.4 4.7 %shard_map.78 = (f32[512,1024]{1,0:T(8,128)}, f32[1,512]{1,0:T(1,128)}) custom-call(bf16[512,384]{1,0:T(8,128)(2,1)} %get-tuple-element.7.gain_ref, bf16[384,1024]{1,0:T(8,128)(2,1)} %get-tuple-element.8.pc_ref, f32[1,512]{1,0:T(1,128)} %get-tuple-element.9.shift_ref, f32[1,512]{1,0:T(1,128)} %bitcast.5, f32[512,1024]{1,0:T(8,128)} %cov_ref.1), custom_call_target="tpu_custom_call" | custom-call | tf_op jit(solution)/shard_map/pallas_call | solution.py:133

commit v4 on v3

--- a/solution.py
+++ b/solution.py
@@ -127,14 +127,14 @@
 
 def update(gain, panel, shift, mean, cov, steps=4):
     n, m = cov.shape
-    rows = n // steps
+    width = m // steps
     whole = lambda *shape: pl.BlockSpec(shape, lambda i: (0,) * len(shape))
-    cut = lambda width: pl.BlockSpec((rows, width), lambda i: (i, 0))
+    cut = lambda rows: pl.BlockSpec((rows, width), lambda i: (0, i))
     return pl.pallas_call(
         update_kernel,
         grid=(steps,),
-        in_specs=[cut(gain.shape[1]), whole(*panel.shape), whole(1, n), whole(1, n), cut(m)],
-        out_specs=[cut(m), whole(1, n)],
+        in_specs=[whole(*gain.shape), cut(panel.shape[0]), whole(1, n), whole(1, n), cut(n)],
+        out_specs=[cut(n), whole(1, n)],
         out_shape=[jax.ShapeDtypeStruct((n, m), jnp.float32), jax.ShapeDtypeStruct((1, n), jnp.float32)],
     )(gain, panel, shift, mean, cov)
 
@@ -215,6 +215,47 @@
 
     lax.fori_loop(1, nc, start_ctx, 0)
 
+    for load in loads[:1] + loads[2:]:
+        load.wait()
+
+    def wait_ctx(t, _):
+        plane_arrival(ctx_all, 0, (c + t) % nc).wait_recv()
+        return 0
+
+    lax.fori_loop(1, nc, wait_ctx, 0)
+    tokens, depth = ctx_m.shape
+    half = tokens // 2
+    ctx_m[...] = ctx_all[...].astype(jnp.float32).reshape(tokens, depth).astype(jnp.bfloat16)
+
+    def line_copy(src, dst, phase, t):
+        return remote(src, dst, send.at[phase, t], recv.at[phase, z], at((z + t) % nz, h, c))
+
+    def line_arrival(buf, phase, src):
+        return remote(buf.at[src], buf.at[src], send.at[phase, 0], recv.at[phase, src], at(z, other, c))
+
+    def swap_x(block):
+        theirs = pl.ds(pl.multiple_of(other * half, half), half)
+        return remote(x_send.at[block, theirs], x_recv.at[block], pair_s.at[block], pair_r.at[block], at(z, other, c))
+
+    for block in range(4):
+        x_send[block] = jnp.dot(ctx_m[...], w_v[:, block * 256 : block * 256 + 256], preferred_element_type=jnp.float32)
+        swap_x(block).start()
+    own_rows = pl.ds(pl.multiple_of(h * half, half), half)
+    for block in range(4):
+        swap_x(block).wait_recv()
+        both = x_send[block, own_rows, :] + x_recv[block]
+        z_send[block] = both
+        z_code[block] = coded_sum(both).reshape(4, 16, 256)
+    pl.semaphore_wait(near, 2)
+
+    def start_z(t, _):
+        t = far_first(t, nz)
+        k = (z + t) % nz
+        line_copy(z_code.at[k % 4, k // 4], z_recv.at[z], 1, t).start()
+        return 0
+
+    lax.fori_loop(0, nz - 1, start_z, 0)
+
     loads[1].wait()
     rows = cov_v.shape[0]
     for i in range(rows // 128):
@@ -222,59 +263,6 @@
         hi, mid, _ = split3(cov_v[cut, :].T)
         c_hi[:, cut] = hi
         c_mid[:, cut] = mid
-    for load in loads[:1] + loads[2:]:
-        load.wait()
-
-    def wait_ctx(t, _):
-        plane_arrival(ctx_all, 0, (c + t) % nc).wait_recv()
-        return 0
-
-    lax.fori_loop(1, nc, wait_ctx, 0)
-    tokens, depth = ctx_m.shape
-    half = tokens // 2
-    ctx_m[...] = ctx_all[...].astype(jnp.float32).reshape(tokens, depth).astype(jnp.bfloat16)
-
-    theirs = ctx_m[pl.ds(pl.multiple_of(other * half, half), half), :]
-    mine = ctx_m[pl.ds(pl.multiple_of(h * half, half), half), :]
-
-    def line_copy(src, dst, phase, t):
-        return remote(src, dst, send.at[phase, t], recv.at[phase, z], at((z + t) % nz, h, c))
-
-    def line_arrival(buf, phase, src):
-        return remote(buf.at[src], buf.at[src], send.at[phase, 0], recv.at[phase, src], at(z, other, c))
-
-    def columns(block):
-        return w_v[:, pl.ds(pl.multiple_of(block * 256, 256), 256)]
-
-    def swap_x(block):
-        return remote(x_send.at[block], x_recv.at[block], pair_s.at[block], pair_r.at[block], at(z, other, c))
-
-    order = [(z + t) % 4 for t in (0, 1, 3, 2)]
-    for block in order:
-        x_send[block] = jnp.dot(theirs, columns(block), preferred_element_type=jnp.float32)
-        swap_x(block).start()
-    for t, block in zip((0, 1, 3, 2), order):
-        z_send[block] = jnp.dot(mine, columns(block), preferred_element_type=jnp.float32)
-    pl.semaphore_wait(near, 2)
-    for t, block in zip((0, 1, 3, 2), order):
-        swap_x(block).wait_recv()
-        both = z_send[block] + x_recv[block]
-        z_send[block] = both
-        z_code[block] = coded_sum(both).reshape(4, 16, 256)
-
-        def start_z(i, _):
-            step = t + (i * 4 + 8) % nz
-            row = (z + step) % nz // 4
-
-            @pl.when(step > 0)
-            def _():
-                remote(
-                    z_code.at[block, row], z_recv.at[z], send.at[1, step], recv.at[1, z], at((z + step) % nz, h, c)
-                ).start()
-
-            return 0
-
-        lax.fori_loop(0, 4, start_z, 0)
 
     def add_z(t, acc):
         zz = (z + near_first(t, nz)) % nz
@@ -527,11 +515,13 @@
         pc_out[tokens : 2 * tokens, cut] = mid
         pc_out[2 * tokens :, cut] = hi
     pr = pr_all[...].reshape(tokens, width)
-    pr_t = pr.T
+    rh, rm, _ = split3(pr.T)
+    pr_t = jnp.concatenate([rh, rh, rm], 1)
     for lo in range(96, 128, 16):
         blocks = eliminated(blocks, lo, 16)
     inv = jnp.concatenate(blocks, 0)
-    gain = jnp.dot(pr_t, inv, precision=HI, preferred_element_type=jnp.float32)
+    ih, im, _ = split3(inv)
+    gain = jnp.dot(pr_t, jnp.concatenate([ih, im, ih], 0), preferred_element_type=jnp.float32)
     hi, mid, _ = split3(gain)
     gain_out[:, :tokens] = hi
     gain_out[:, tokens : 2 * tokens] = hi
@@ -590,7 +580,7 @@
     scratch = [
         vmem((nc, rows_here, depth), bf16), vmem((b, depth), bf16), vmem((depth, m), bf16), vmem((1, m), f32),
         vmem((n, m), f32), vmem((1, n), f32), vmem((1, b), f32), vmem((m, n), bf16), vmem((m, n), bf16),
-        vmem((4, b // 2, 256), f32), vmem((4, b // 2, 256), f32), vmem((4, b // 2, 256), f32),
+        vmem((4, b, 256), f32), vmem((4, b // 2, 256), f32), vmem((4, b // 2, 256), f32),
         vmem((4, 4, 16, 256), bf16), vmem((nz, 16, 256), bf16),
         vmem((16, 256), bf16), vmem((2 * nz, 16, 256), bf16), vmem((16, 16, 256), bf16),
         vmem((nc, 8, n), f32), vmem((nc, 8, n), f32), vmem((8, n), f32), vmem((1, 8, n), bf16),

time: 86.3 us -> 83 us (0.962)
  Pallas kernels: 85.4 us -> 82.2 us
    pallas_call x1, Pallas kernels: 80.7 us -> 77.5 us  [exchange(): pl.pallas_call(exchange_kernel, in_specs=[pl.BlockSpec(memory_space=pl.AN...]
where the time goes in v4:
time: 83 us; the launch traced here: 82.8 us
  Pallas kernels  82.2 us (99%)
    pallas_call x1, Pallas kernels, exchange(): pl.pallas_call(exchange_kernel, in_specs=[pl.BlockSpec(memory_space=pl.AN...  77.5 us
    pallas_call x1, Pallas kernels, update(): pl.pallas_call(update_kernel, grid=(steps,), in_specs=[whole(*gain.shape)...  4.64 us

profile of v4, /device:TPU:1, one launch (start us, length us, event | category | flops | bytes accessed | tf_op | source)
XLA Modules:
  0.0 82.8 jit_solution(16693769062838932178)
XLA Ops:
  0.6 77.5 %shard_map.77 = (bf16[512,384]{1,0:T(8,128)(2,1)}, bf16[384,1024]{1,0:T(8,128)(2,1)}, f32[1,512]{1,0:T(1,128)}) custom-call(bf16[8,256]{1,0:T(8,128)(2,1)} %ctx_hbm.1, bf16[256,1024]{1,0:T(8,128)(2,1)} %w_hbm.1, f32[1,1024]{1,0:T(1,128)} %bitcast.6, f32[512,1024]{1,0:T(8,128)} %cov_ref.1, f32[1,512]{1,0:T(1,128)} %bitcast.4, f32[1,128]{1,0:T(1,128)} %bitcast.7), custom_call_target="tpu_custom_call" | custom-call | tf_op jit(solution)/shard_map/pallas_call | solution.py:593
  78.2 4.6 %shard_map.78 = (f32[512,1024]{1,0:T(8,128)}, f32[1,512]{1,0:T(1,128)}) custom-call(bf16[512,384]{1,0:T(8,128)(2,1)} %get-tuple-element.7.gain_ref, bf16[384,1024]{1,0:T(8,128)(2,1)} %get-tuple-element.8.pc_ref, f32[1,512]{1,0:T(1,128)} %get-tuple-element.9.shift_ref, f32[1,512]{1,0:T(1,128)} %bitcast.5, f32[512,1024]{1,0:T(8,128)} %cov_ref.1), custom_call_target="tpu_custom_call" | custom-call | tf_op jit(solution)/shard_map/pallas_call | solution.py:133

commit v5 on v4

--- a/solution.py
+++ b/solution.py
@@ -140,7 +140,7 @@
 
 
 def far_first(t, n):
-    return n // 2 + (1 - 2 * (t % 2)) * ((t + 1) // 2)
+    return n // 2 + (1 - 2 * lax.rem(t, 2)) * lax.div(t + 1, 2)
 
 
 def near_first(t, n):
@@ -152,13 +152,13 @@
     gain_out, pc_out, shift_out,
     ctx_all, ctx_m, w_v, bias_v, cov_v, mean_v, rew_v, c_hi, c_mid,
     x_send, x_recv, z_send, z_code, z_recv, phi_s, phi_c, phi_r,
-    pp_send, pp_recv, p_own, p_code, gz_s, gz_r, pz_s, pz_r, g_s, g_all, pred_s, pred_r,
+    pp_send, pp_recv, p_code, gz_s, gz_r, pz_s, pz_r, g_s, g_all, pred_s, pred_r,
     pr_all, p_z, pc_all,
     local, near, pair_s, pair_r, send, recv, mate, send_pc, recv_pc, send_g, recv_g,
 ):
     nz, nc, nb = z_recv.shape[0], ctx_all.shape[0], 4
     r, c = lax.axis_index("row"), lax.axis_index("col")
-    z, h = r // 2, r % 2
+    z, h = lax.div(r, 2), lax.rem(r, 2)
     other = 1 - h
 
     def at(zz, hh, cc):
@@ -186,25 +186,25 @@
         pl.semaphore_signal(barrier, inc=1, device_id=where, device_id_type=MESH)
 
     def greet_plane(t, _):
-        greet(at(z, h, (c + t) % nc))
+        greet(at(z, h, lax.rem(c + t, nc)))
         return 0
 
     def greet_line(t, _):
-        greet(at((z + t) % nz, h, c))
-        greet(at((z - t + nz) % nz, h, c))
-        greet(at((z + t) % nz, other, c))
-        greet(at((z - t + nz) % nz, other, c))
+        greet(at(lax.rem(z + t, nz), h, c))
+        greet(at(lax.rem(z - t + nz, nz), h, c))
+        greet(at(lax.rem(z + t, nz), other, c))
+        greet(at(lax.rem(z - t + nz, nz), other, c))
         return 0
 
     lax.fori_loop(1, nc, greet_plane, 0)
     lax.fori_loop(1, nb + 1, greet_line, 0)
     greet(at(z, other, c))
     pl.semaphore_wait(barrier, nc - 1 + 4 * nb + 1)
-    pl.semaphore_signal(near, inc=1, device_id=at((z + nb) % nz, h, c), device_id_type=MESH)
-    pl.semaphore_signal(near, inc=1, device_id=at((z - nb + nz) % nz, h, c), device_id_type=MESH)
+    pl.semaphore_signal(near, inc=1, device_id=at(lax.rem(z + nb, nz), h, c), device_id_type=MESH)
+    pl.semaphore_signal(near, inc=1, device_id=at(lax.rem(z - nb + nz, nz), h, c), device_id_type=MESH)
 
     def ctx_copy(t):
-        return remote(ctx_hbm, ctx_all.at[c], send.at[0, t], recv.at[0, c], at(z, h, (c + t) % nc))
+        return remote(ctx_hbm, ctx_all.at[c], send.at[0, t], recv.at[0, c], at(z, h, lax.rem(c + t, nc)))
 
     def plane_arrival(buf, phase, src):
         return remote(buf.at[src], buf.at[src], send.at[phase, 0], recv.at[phase, src], at(z, other, c))
@@ -219,7 +219,7 @@
         load.wait()
 
     def wait_ctx(t, _):
-        plane_arrival(ctx_all, 0, (c + t) % nc).wait_recv()
+        plane_arrival(ctx_all, 0, lax.rem(c + t, nc)).wait_recv()
         return 0
 
     lax.fori_loop(1, nc, wait_ctx, 0)
@@ -228,7 +228,7 @@
     ctx_m[...] = ctx_all[...].astype(jnp.float32).reshape(tokens, depth).astype(jnp.bfloat16)
 
     def line_copy(src, dst, phase, t):
-        return remote(src, dst, send.at[phase, t], recv.at[phase, z], at((z + t) % nz, h, c))
+        return remote(src, dst, send.at[phase, t], recv.at[phase, z], at(lax.rem(z + t, nz), h, c))
 
     def line_arrival(buf, phase, src):
         return remote(buf.at[src], buf.at[src], send.at[phase, 0], recv.at[phase, src], at(z, other, c))
@@ -250,8 +250,8 @@
 
     def start_z(t, _):
         t = far_first(t, nz)
-        k = (z + t) % nz
-        line_copy(z_code.at[k % 4, k // 4], z_recv.at[z], 1, t).start()
+        k = lax.rem(z + t, nz)
+        line_copy(z_code.at[lax.rem(k, 4), lax.div(k, 4)], z_recv.at[z], 1, t).start()
         return 0
 
     lax.fori_loop(0, nz - 1, start_z, 0)
@@ -265,12 +265,12 @@
         c_mid[:, cut] = mid
 
     def add_z(t, acc):
-        zz = (z + near_first(t, nz)) % nz
+        zz = lax.rem(z + near_first(t, nz), nz)
         line_arrival(z_recv, 1, zz).wait_recv()
         return acc + sum_from(z_recv[zz])
 
-    kb = z % 4
-    own = z_send[kb, pl.ds(pl.multiple_of(z // 4 * 16, 16), 16), :]
+    kb = lax.rem(z, 4)
+    own = z_send[kb, pl.ds(pl.multiple_of(lax.div(z, 4) * 16, 16), 16), :]
     total = lax.fori_loop(0, nz - 1, add_z, own)
     total = total + bias_v[:, pl.ds(pl.multiple_of(kb * 256, 256), 256)]
     phi = jnp.tanh(total).astype(jnp.bfloat16)
@@ -287,15 +287,15 @@
         return remote(phi_c.at[h * nz + k], phi_c.at[h * nz + k], mate.at[0, k], mate.at[1, k], at(z, other, c))
 
     def plane_copy(src, dst, phase, t):
-        return remote(src, dst, send.at[phase, t], recv.at[phase, c], at(z, h, (c + t) % nc))
+        return remote(src, dst, send.at[phase, t], recv.at[phase, c], at(z, h, lax.rem(c + t, nc)))
 
     holder = c == z
 
     def push(core, k):
-        column = k % 4
-        slot = core * 8 + k // 4 * 2 + column % 2
-
-        @pl.when(jnp.logical_and(holder, column // 2 == h))
+        column = lax.rem(k, 4)
+        slot = core * 8 + lax.div(k, 4) * 2 + lax.rem(column, 2)
+
+        @pl.when(jnp.logical_and(holder, lax.div(column, 2) == h))
         def _():
             phi_r[slot] = phi_c[core * nz + k]
 
@@ -308,7 +308,7 @@
     push(h, z)
 
     def pass_mate(t, _):
-        zz = (z + near_first(t, nz)) % nz
+        zz = lax.rem(z + near_first(t, nz), nz)
         remote(phi_s, phi_c.at[h * nz + zz], send.at[2, 0], recv.at[2, zz], at(z, other, c)).wait_recv()
         mate_copy(zz).start()
         push(h, zz)
@@ -317,8 +317,7 @@
     lax.fori_loop(0, nz - 1, pass_mate, 0)
 
     def wait_mate(t, _):
-        k = (z + near_first(t - 1, nz)) % nz
-        k = jnp.where(t == 0, z, k)
+        k = lax.rem(z + near_first(t - 1, nz), nz)
         i = other * nz + k
         remote(phi_c.at[i], phi_c.at[i], mate.at[0, k], mate.at[1, k], at(z, other, c)).wait_recv()
         push(other, k)
@@ -332,10 +331,10 @@
         for term in (c_hi, c_mid):
             prod = jnp.dot(lhs, term[k * 256 : k * 256 + 256, :], preferred_element_type=jnp.float32)
             part = prod if part is None else part + prod
-    pp_send[...] = part.reshape(pp_send.shape)
+    pp_send[...] = coded_panel(part).reshape(pp_send.shape)
 
     def start_pp(t, _):
-        plane_copy(pp_send.at[(c + t) % nc], pp_recv.at[c], 5, t).start()
+        plane_copy(pp_send.at[lax.rem(c + t, nc)], pp_recv.at[c], 5, t).start()
         return 0
 
     lax.fori_loop(1, nc, start_pp, 0)
@@ -349,7 +348,7 @@
         plane_arrival(phi_r, 4, c).wait_recv()
 
     def start_row(t, _):
-        @pl.when((c + t) % nc != z)
+        @pl.when(lax.rem(c + t, nc) != z)
         def _():
             pass_row(t).start()
 
@@ -360,17 +359,16 @@
     def wait_row(t, _):
         @pl.when(jnp.logical_not(holder))
         def _():
-            plane_arrival(phi_r, 4, (c + t) % nc).wait_recv()
+            plane_arrival(phi_r, 4, lax.rem(c + t, nc)).wait_recv()
 
         return 0
 
     def wait_pp(t, _):
-        plane_arrival(pp_recv, 5, (c + t) % nc).wait_recv()
+        plane_arrival(pp_recv, 5, lax.rem(c + t, nc)).wait_recv()
         return 0
 
     lax.fori_loop(1, nc, wait_pp, 0)
-    p_mine = jnp.sum(pp_recv[...], axis=0)
-    p_own[...] = p_mine
+    p_mine = jnp.sum(panel_from(pp_recv[...]), axis=0)
     p_code[0] = coded_panel(p_mine)
     lax.fori_loop(1, nc, wait_row, 0)
 
@@ -408,7 +406,7 @@
     lax.fori_loop(0, nz - 1, start_pz, 0)
 
     def wait_gz(t, _):
-        zz = (z + t) % nz
+        zz = lax.rem(z + t, nz)
         line_arrival(gz_r, 7, zz).wait_recv()
         line_arrival(pz_r, 8, zz).wait_recv()
         return 0
@@ -420,7 +418,7 @@
     swap_pred.start()
 
     def g_copy(t, core):
-        return remote(g_s, g_all.at[h, c], send_g.at[core, t], recv_g.at[h, c], at(z, core, (c + t) % nc))
+        return remote(g_s, g_all.at[h, c], send_g.at[core, t], recv_g.at[h, c], at(z, core, lax.rem(c + t, nc)))
 
     def g_arrival(core, p):
         return remote(g_s, g_all.at[core, p], send_g.at[0, 0], recv_g.at[core, p], at(z, other, c))
@@ -437,14 +435,14 @@
     g_all[h, c] = g_s[...]
 
     def start_pr(t, _):
-        plane_copy(p_own, pr_all.at[c], 6, t).start()
+        plane_copy(p_code.at[0], pr_all.at[c], 6, t).start()
         return 0
 
     lax.fori_loop(1, nc, start_pr, 0)
-    pr_all[c] = p_own[...]
+    pr_all[c] = p_code[0]
 
     def wait_g(t, _):
-        p = (c + t) % nc
+        p = lax.rem(c + t, nc)
 
         @pl.when(t > 0)
         def _():
@@ -457,15 +455,14 @@
     eye = (lax.broadcasted_iota(jnp.int32, (tokens, tokens), 0) == lax.broadcasted_iota(jnp.int32, (tokens, tokens), 1)).astype(jnp.float32)
     g = (g_all[0] + g_all[1]).reshape(tokens, tokens) + eye
     blocks = [g[8 * i : 8 * i + 8] for i in range(tokens // 8)]
-    for lo in range(0, 48, 16):
+    for lo in range(0, 32, 16):
         blocks = eliminated(blocks, lo, 16)
 
     def col_copy(zz, core):
         return remote(p_z.at[zz], pc_all.at[h, c], send_pc.at[core, zz], recv_pc.at[h, c], at(z, core, zz))
 
     def pass_pz(t, _):
-        zz = (z + near_first(t - 1, nz)) % nz
-        zz = jnp.where(t == 0, z, zz)
+        zz = lax.rem(z + near_first(t - 1, nz), nz)
 
         @pl.when(t > 0)
         def _():
@@ -484,18 +481,18 @@
 
     lax.fori_loop(0, nz, pass_pz, 0)
 
-    for lo in range(48, 96, 16):
+    for lo in range(32, 96, 16):
         blocks = eliminated(blocks, lo, 16)
 
     def wait_last(t, _):
-        p = (c + t) % nc
+        p = lax.rem(c + t, nc)
         plane_arrival(pr_all, 6, p).wait_recv()
         return 0
 
     lax.fori_loop(1, nc, wait_last, 0)
 
     def wait_pc(t, _):
-        p = (c + t) % nc
+        p = lax.rem(c + t, nc)
 
         @pl.when(t > 0)
         def _():
@@ -514,7 +511,7 @@
         pc_out[:tokens, cut] = hi
         pc_out[tokens : 2 * tokens, cut] = mid
         pc_out[2 * tokens :, cut] = hi
-    pr = pr_all[...].reshape(tokens, width)
+    pr = panel_from(pr_all[...]).reshape(tokens, width)
     rh, rm, _ = split3(pr.T)
     pr_t = jnp.concatenate([rh, rh, rm], 1)
     for lo in range(96, 128, 16):
@@ -535,15 +532,15 @@
 
     def sent(t, _):
         ctx_copy(t).wait_send()
-        remote(phi_s, z_recv.at[z], send.at[1, t], recv.at[1, z], at((z + t) % nz, h, c)).wait_send()
+        remote(phi_s, z_recv.at[z], send.at[1, t], recv.at[1, z], at(lax.rem(z + t, nz), h, c)).wait_send()
         line_copy(phi_s, phi_c.at[h * nz + z], 2, t).wait_send()
 
-        @pl.when((c + t) % nc != z)
+        @pl.when(lax.rem(c + t, nc) != z)
         def _():
             pass_row(t).wait_send()
 
-        plane_copy(pp_send.at[(c + t) % nc], pp_recv.at[c], 5, t).wait_send()
-        plane_copy(p_own, pr_all.at[c], 6, t).wait_send()
+        plane_copy(pp_send.at[lax.rem(c + t, nc)], pp_recv.at[c], 5, t).wait_send()
+        plane_copy(p_code.at[0], pr_all.at[c], 6, t).wait_send()
         line_copy(gz_s, gz_r.at[z], 7, t).wait_send()
         line_copy(pz_s, pz_r.at[z], 8, t).wait_send()
         line_copy(p_code.at[0], p_z.at[z], 9, t).wait_send()
@@ -583,10 +580,10 @@
         vmem((4, b, 256), f32), vmem((4, b // 2, 256), f32), vmem((4, b // 2, 256), f32),
         vmem((4, 4, 16, 256), bf16), vmem((nz, 16, 256), bf16),
         vmem((16, 256), bf16), vmem((2 * nz, 16, 256), bf16), vmem((16, 16, 256), bf16),
-        vmem((nc, 8, n), f32), vmem((nc, 8, n), f32), vmem((8, n), f32), vmem((1, 8, n), bf16),
+        vmem((nc, 8, n), bf16), vmem((nc, 8, n), bf16), vmem((1, 8, n), bf16),
         vmem((8, b), f32), vmem((nz, 8, b), f32), vmem((1, b), f32), vmem((nz, 1, b), f32), vmem((8, b), f32), vmem((2, nc, 8, b), f32),
         vmem((1, b), f32), vmem((1, b), f32),
-        vmem((nc, 8, n), f32), vmem((nz, 8, n), bf16), vmem((2, nc, 8, n), bf16),
+        vmem((nc, 8, n), bf16), vmem((nz, 8, n), bf16), vmem((2, nc, 8, n), bf16),
         sem.DMA((6,)), sem.REGULAR, sem.DMA((5,)), sem.DMA((5,)), sem.DMA((10, 16)), sem.DMA((10, 16)), sem.DMA((2, 16)),
         sem.DMA((2, 16)), sem.DMA((2, 16)), sem.DMA((2, 16)), sem.DMA((2, 16)),
     ]

time: 83 us -> 81.4 us (0.981)
  Pallas kernels: 82.2 us -> 80.6 us
    pallas_call x1, Pallas kernels: 77.5 us -> 76 us  [exchange(): pl.pallas_call(exchange_kernel, in_specs=[pl.BlockSpec(memory_space=pl.AN...]
where the time goes in v5:
time: 81.4 us; the launch traced here: 81.2 us
  Pallas kernels  80.6 us (99%)
    pallas_call x1, Pallas kernels, exchange(): pl.pallas_call(exchange_kernel, in_specs=[pl.BlockSpec(memory_space=pl.AN...  76 us
    pallas_call x1, Pallas kernels, update(): pl.pallas_call(update_kernel, grid=(steps,), in_specs=[whole(*gain.shape)...  4.64 us

profile of v5, /device:TPU:1, one launch (start us, length us, event | category | flops | bytes accessed | tf_op | source)
XLA Modules:
  0.0 81.2 jit_solution(6573089327840553355)
XLA Ops:
  0.6 76.0 %shard_map.77 = (bf16[512,384]{1,0:T(8,128)(2,1)}, bf16[384,1024]{1,0:T(8,128)(2,1)}, f32[1,512]{1,0:T(1,128)}) custom-call(bf16[8,256]{1,0:T(8,128)(2,1)} %ctx_hbm.1, bf16[256,1024]{1,0:T(8,128)(2,1)} %w_hbm.1, f32[1,1024]{1,0:T(1,128)} %bitcast.6, f32[512,1024]{1,0:T(8,128)} %cov_ref.1, f32[1,512]{1,0:T(1,128)} %bitcast.4, f32[1,128]{1,0:T(1,128)} %bitcast.7), custom_call_target="tpu_custom_call" | custom-call | tf_op jit(solution)/shard_map/pallas_call | solution.py:590
  76.6 4.6 %shard_map.78 = (f32[512,1024]{1,0:T(8,128)}, f32[1,512]{1,0:T(1,128)}) custom-call(bf16[512,384]{1,0:T(8,128)(2,1)} %get-tuple-element.7.gain_ref, bf16[384,1024]{1,0:T(8,128)(2,1)} %get-tuple-element.8.pc_ref, f32[1,512]{1,0:T(1,128)} %get-tuple-element.9.shift_ref, f32[1,512]{1,0:T(1,128)} %bitcast.5, f32[512,1024]{1,0:T(8,128)} %cov_ref.1), custom_call_target="tpu_custom_call" | custom-call | tf_op jit(solution)/shard_map/pallas_call | solution.py:133

commit v6 on v5

--- a/solution.py
+++ b/solution.py
@@ -125,7 +125,7 @@
         outm_ref[...] = mean_ref[...] + shift_ref[...]
 
 
-def update(gain, panel, shift, mean, cov, steps=4):
+def update(gain, panel, shift, mean, cov, steps=2):
     n, m = cov.shape
     width = m // steps
     whole = lambda *shape: pl.BlockSpec(shape, lambda i: (0,) * len(shape))
@@ -136,6 +136,7 @@
         in_specs=[whole(*gain.shape), cut(panel.shape[0]), whole(1, n), whole(1, n), cut(n)],
         out_specs=[cut(n), whole(1, n)],
         out_shape=[jax.ShapeDtypeStruct((n, m), jnp.float32), jax.ShapeDtypeStruct((1, n), jnp.float32)],
+        compiler_params=pltpu.CompilerParams(vmem_limit_bytes=16 << 20),
     )(gain, panel, shift, mean, cov)
 
 
@@ -192,14 +193,12 @@
     def greet_line(t, _):
         greet(at(lax.rem(z + t, nz), h, c))
         greet(at(lax.rem(z - t + nz, nz), h, c))
-        greet(at(lax.rem(z + t, nz), other, c))
-        greet(at(lax.rem(z - t + nz, nz), other, c))
         return 0
 
     lax.fori_loop(1, nc, greet_plane, 0)
     lax.fori_loop(1, nb + 1, greet_line, 0)
     greet(at(z, other, c))
-    pl.semaphore_wait(barrier, nc - 1 + 4 * nb + 1)
+    pl.semaphore_wait(barrier, nc - 1 + 2 * nb + 1)
     pl.semaphore_signal(near, inc=1, device_id=at(lax.rem(z + nb, nz), h, c), device_id_type=MESH)
     pl.semaphore_signal(near, inc=1, device_id=at(lax.rem(z - nb + nz, nz), h, c), device_id_type=MESH)
 
@@ -215,6 +214,15 @@
 
     lax.fori_loop(1, nc, start_ctx, 0)
 
+    def covariance_terms(first, last):
+        for i in range(first, last):
+            cut = slice(i * 128, i * 128 + 128)
+            hi, mid, _ = split3(cov_v[cut, :].T)
+            c_hi[:, cut] = hi
+            c_mid[:, cut] = mid
+
+    loads[1].wait()
+    covariance_terms(0, 2)
     for load in loads[:1] + loads[2:]:
         load.wait()
 
@@ -256,13 +264,7 @@
 
     lax.fori_loop(0, nz - 1, start_z, 0)
 
-    loads[1].wait()
-    rows = cov_v.shape[0]
-    for i in range(rows // 128):
-        cut = slice(i * 128, i * 128 + 128)
-        hi, mid, _ = split3(cov_v[cut, :].T)
-        c_hi[:, cut] = hi
-        c_mid[:, cut] = mid
+    covariance_terms(2, 4)
 
     def add_z(t, acc):
         zz = lax.rem(z + near_first(t, nz), nz)
@@ -441,6 +443,29 @@
     lax.fori_loop(1, nc, start_pr, 0)
     pr_all[c] = p_code[0]
 
+    def col_copy(zz, core):
+        return remote(p_z.at[zz], pc_all.at[h, c], send_pc.at[core, zz], recv_pc.at[h, c], at(z, core, zz))
+
+    def pass_pz(t, _):
+        zz = lax.rem(z + near_first(t - 1, nz), nz)
+
+        @pl.when(t > 0)
+        def _():
+            line_arrival(p_z, 9, zz).wait_recv()
+
+        @pl.when(zz == c)
+        def _():
+            pc_all[h, c] = p_z[zz]
+
+        @pl.when(zz != c)
+        def _():
+            col_copy(zz, h).start()
+
+        col_copy(zz, other).start()
+        return 0
+
+    lax.fori_loop(0, nz, pass_pz, 0)
+
     def wait_g(t, _):
         p = lax.rem(c + t, nc)
 
@@ -457,29 +482,6 @@
     blocks = [g[8 * i : 8 * i + 8] for i in range(tokens // 8)]
     for lo in range(0, 32, 16):
         blocks = eliminated(blocks, lo, 16)
-
-    def col_copy(zz, core):
-        return remote(p_z.at[zz], pc_all.at[h, c], send_pc.at[core, zz], recv_pc.at[h, c], at(z, core, zz))
-
-    def pass_pz(t, _):
-        zz = lax.rem(z + near_first(t - 1, nz), nz)
-
-        @pl.when(t > 0)
-        def _():
-            line_arrival(p_z, 9, zz).wait_recv()
-
-        @pl.when(zz == c)
-        def _():
-            pc_all[h, c] = p_z[zz]
-
-        @pl.when(zz != c)
-        def _():
-            col_copy(zz, h).start()
-
-        col_copy(zz, other).start()
-        return 0
-
-    lax.fori_loop(0, nz, pass_pz, 0)
 
     for lo in range(32, 96, 16):
         blocks = eliminated(blocks, lo, 16)
@@ -589,20 +591,20 @@
     ]
     return pl.pallas_call(
         exchange_kernel,
-        in_specs=[pl.BlockSpec(memory_space=pl.ANY)] * 6,
+        in_specs=[pl.BlockSpec(memory_space=pltpu.HBM)] * 6,
         out_specs=[pl.BlockSpec(memory_space=pltpu.VMEM)] * 3,
         out_shape=[
             jax.ShapeDtypeStruct((n, 3 * b), bf16), jax.ShapeDtypeStruct((3 * b, m), bf16), jax.ShapeDtypeStruct((1, n), f32),
         ],
         scratch_shapes=scratch,
-        compiler_params=pltpu.CompilerParams(collective_id=0, has_side_effects=True),
-    )(context, weight, bias, covariance, mean, rewards)
+        compiler_params=pltpu.CompilerParams(collective_id=0, has_side_effects=True, vmem_limit_bytes=28 << 20),
+    )(*(pltpu.with_memory_space_constraint(x, pltpu.HBM) for x in (context, weight, bias, covariance, mean, rewards)))
 
 
 def per_device(context, weight, feature_bias, covariance, prior_mean, rewards):
     mean = prior_mean.reshape(1, -1)
     gain, panel, shift = exchange(context, weight, feature_bias.reshape(1, -1), covariance, mean, rewards.reshape(1, -1))
-    cov, mean = update(gain, panel, shift, mean, covariance)
+    cov, mean = update(gain, panel, shift, mean, pltpu.with_memory_space_constraint(covariance, pltpu.HBM))
     return cov, mean.reshape(-1)
 
 

time: 81.4 us -> 79.1 us (0.972)
  Pallas kernels: 80.6 us -> 78.3 us
    pallas_call x1, Pallas kernels: 4.64 us -> 3.12 us  [update(): pl.pallas_call(update_kernel, grid=(steps,), in_specs=[whole(*gain.shape)...]
where the time goes in v6:
time: 79.1 us; the launch traced here: 78.9 us
  Pallas kernels  78.3 us (99%)
    pallas_call x1, Pallas kernels, exchange(): pl.pallas_call(exchange_kernel, in_specs=[pl.BlockSpec(memory_space=pltpu...  75.2 us
    pallas_call x1, Pallas kernels, update(): pl.pallas_call(update_kernel, grid=(steps,), in_specs=[whole(*gain.shape)...  3.12 us

profile of v6, /device:TPU:1, one launch (start us, length us, event | category | flops | bytes accessed | tf_op | source)
XLA Modules:
  0.0 78.9 jit_solution(18429283289428409503)
XLA Ops:
  0.6 0.0 copy-start
  0.6 75.2 %shard_map.77 = (bf16[512,384]{1,0:T(8,128)(2,1)S(1)}, bf16[384,1024]{1,0:T(8,128)(2,1)S(1)}, f32[1,512]{1,0:T(1,128)S(1)}) custom-call(bf16[8,256]{1,0:T(8,128)(2,1)} %ctx_hbm.1, bf16[256,1024]{1,0:T(8,128)(2,1)} %w_hbm.1, f32[1,1024]{1,0:T(1,128)} %bitcast.6, f32[512,1024]{1,0:T(8,128)} %cov_ref.1, f32[1,512]{1,0:T(1,128)} %bitcast.4, f32[1,128]{1,0:T(1,128)} %bitcast.7), custom_call_target="tpu_custom_call" | custom-call | tf_op jit(solution)/shard_map/pallas_call | solution.py:592
  75.8 0.0 copy-done
  75.8 3.1 %shard_map.78 = (f32[512,1024]{1,0:T(8,128)}, f32[1,512]{1,0:T(1,128)}) custom-call(bf16[512,384]{1,0:T(8,128)(2,1)S(1)} %get-tuple-element.7.gain_ref, bf16[384,1024]{1,0:T(8,128)(2,1)S(1)} %get-tuple-element.8.pc_ref, f32[1,512]{1,0:T(1,128)S(1)} %get-tuple-element.9.shift_ref, f32[1,512]{1,0:T(1,128)S(1)} %bitcast.5, f32[512,1024]{1,0:T(8,128)} %cov_ref.1), custom_call_target="tpu_custom_call" | custom-call | tf_op jit(solution)/shard_map/pallas_call | solution.py:133
Async XLA Ops:
  0.6 75.2 %copy-start = (f32[512]{0:T(512)S(1)}, f32[512]{0:T(512)}, u32[]{:S(2)}) copy-start(f32[512]{0:T(512)} %param.10) | copy-start | bytes 6148

commit v7 on v6

--- a/solution.py
+++ b/solution.py
@@ -221,8 +221,6 @@
             c_hi[:, cut] = hi
             c_mid[:, cut] = mid
 
-    loads[1].wait()
-    covariance_terms(0, 2)
     for load in loads[:1] + loads[2:]:
         load.wait()
 
@@ -264,7 +262,8 @@
 
     lax.fori_loop(0, nz - 1, start_z, 0)
 
-    covariance_terms(2, 4)
+    loads[1].wait()
+    covariance_terms(0, 4)
 
     def add_z(t, acc):
         zz = lax.rem(z + near_first(t, nz), nz)
@@ -407,6 +406,13 @@
 
     lax.fori_loop(0, nz - 1, start_pz, 0)
 
+    def start_pr(t, _):
+        plane_copy(p_code.at[0], pr_all.at[c], 6, t).start()
+        return 0
+
+    lax.fori_loop(1, nc, start_pr, 0)
+    pr_all[c] = p_code[0]
+
     def wait_gz(t, _):
         zz = lax.rem(z + t, nz)
         line_arrival(gz_r, 7, zz).wait_recv()
@@ -435,13 +441,6 @@
 
     lax.fori_loop(0, nc, start_g, 0)
     g_all[h, c] = g_s[...]
-
-    def start_pr(t, _):
-        plane_copy(p_code.at[0], pr_all.at[c], 6, t).start()
-        return 0
-
-    lax.fori_loop(1, nc, start_pr, 0)
-    pr_all[c] = p_code[0]
 
     def col_copy(zz, core):
         return remote(p_z.at[zz], pc_all.at[h, c], send_pc.at[core, zz], recv_pc.at[h, c], at(z, core, zz))

time: 79.1 us -> 77.6 us (0.981)
  Pallas kernels: 78.3 us -> 76.8 us
    pallas_call x1, Pallas kernels: 75.2 us -> 73.7 us  [exchange(): pl.pallas_call(exchange_kernel, in_specs=[pl.BlockSpec(memory_space=pltpu...]
where the time goes in v7:
time: 77.6 us; the launch traced here: 77.5 us
  Pallas kernels  76.8 us (99%)
    pallas_call x1, Pallas kernels, exchange(): pl.pallas_call(exchange_kernel, in_specs=[pl.BlockSpec(memory_space=pltpu...  73.7 us
    pallas_call x1, Pallas kernels, update(): pl.pallas_call(update_kernel, grid=(steps,), in_specs=[whole(*gain.shape)...  3.13 us

profile of v7, /device:TPU:1, one launch (start us, length us, event | category | flops | bytes accessed | tf_op | source)
XLA Modules:
  0.0 77.5 jit_solution(1534834657976564290)
XLA Ops:
  0.6 0.0 copy-start
  0.6 73.7 %shard_map.77 = (bf16[512,384]{1,0:T(8,128)(2,1)S(1)}, bf16[384,1024]{1,0:T(8,128)(2,1)S(1)}, f32[1,512]{1,0:T(1,128)S(1)}) custom-call(bf16[8,256]{1,0:T(8,128)(2,1)} %ctx_hbm.1, bf16[256,1024]{1,0:T(8,128)(2,1)} %w_hbm.1, f32[1,1024]{1,0:T(1,128)} %bitcast.6, f32[512,1024]{1,0:T(8,128)} %cov_ref.1, f32[1,512]{1,0:T(1,128)} %bitcast.4, f32[1,128]{1,0:T(1,128)} %bitcast.7), custom_call_target="tpu_custom_call" | custom-call | tf_op jit(solution)/shard_map/pallas_call | solution.py:591
  74.3 0.0 copy-done
  74.3 3.1 %shard_map.78 = (f32[512,1024]{1,0:T(8,128)}, f32[1,512]{1,0:T(1,128)}) custom-call(bf16[512,384]{1,0:T(8,128)(2,1)S(1)} %get-tuple-element.7.gain_ref, bf16[384,1024]{1,0:T(8,128)(2,1)S(1)} %get-tuple-element.8.pc_ref, f32[1,512]{1,0:T(1,128)S(1)} %get-tuple-element.9.shift_ref, f32[1,512]{1,0:T(1,128)S(1)} %bitcast.5, f32[512,1024]{1,0:T(8,128)} %cov_ref.1), custom_call_target="tpu_custom_call" | custom-call | tf_op jit(solution)/shard_map/pallas_call | solution.py:133
Async XLA Ops:
  0.6 73.7 %copy-start = (f32[512]{0:T(512)S(1)}, f32[512]{0:T(512)}, u32[]{:S(2)}) copy-start(f32[512]{0:T(512)} %param.10) | copy-start | bytes 6148

commit v8 on v7

--- a/solution.py
+++ b/solution.py
@@ -392,7 +392,6 @@
     def start_gz(t, _):
         t = far_first(t, nz)
         line_copy(gz_s, gz_r.at[z], 7, t).start()
-        line_copy(pz_s, pz_r.at[z], 8, t).start()
         return 0
 
     lax.fori_loop(0, nz - 1, start_gz, 0)
@@ -402,6 +401,7 @@
     def start_pz(t, _):
         t = far_first(t, nz)
         line_copy(p_code.at[0], p_z.at[z], 9, t).start()
+        line_copy(pz_s, pz_r.at[z], 8, t).start()
         return 0
 
     lax.fori_loop(0, nz - 1, start_pz, 0)
@@ -412,58 +412,91 @@
 
     lax.fori_loop(1, nc, start_pr, 0)
     pr_all[c] = p_code[0]
+
+    for block in range(4):
+        swap_x(block).wait_send()
+
+    def sent_first(t, _):
+        ctx_copy(t).wait_send()
+        remote(phi_s, z_recv.at[z], send.at[1, t], recv.at[1, z], at(lax.rem(z + t, nz), h, c)).wait_send()
+        line_copy(phi_s, phi_c.at[h * nz + z], 2, t).wait_send()
+        plane_copy(pp_send.at[lax.rem(c + t, nc)], pp_recv.at[c], 5, t).wait_send()
+
+        @pl.when(lax.rem(c + t, nc) != z)
+        def _():
+            pass_row(t).wait_send()
+
+        return 0
+
+    lax.fori_loop(1, nz, sent_first, 0)
+
+    def sent_pieces(t, _):
+        mate_copy(t).wait_send()
+
+        @pl.when(jnp.logical_and(holder, t != z))
+        def _():
+            remote(phi_r.at[t], phi_r.at[t], send.at[3, t], recv.at[4, t], at(z, h, t)).wait_send()
+
+        return 0
+
+    lax.fori_loop(0, nz, sent_pieces, 0)
 
     def wait_gz(t, _):
         zz = lax.rem(z + t, nz)
         line_arrival(gz_r, 7, zz).wait_recv()
-        line_arrival(pz_r, 8, zz).wait_recv()
         return 0
 
     lax.fori_loop(1, nz, wait_gz, 0)
     g_s[...] = jnp.sum(gz_r[...], axis=0)
+
+    def g_copy(t, core):
+        return remote(g_s, g_all.at[h, c], send_g.at[core, t], recv_g.at[h, c], at(z, core, lax.rem(c + t, nc)))
+
+    def g_arrival(core, p):
+        return remote(g_s, g_all.at[core, p], send_g.at[0, 0], recv_g.at[core, p], at(z, other, c))
+
+    def start_g(t, _):
+        @pl.when(t > 0)
+        def _():
+            g_copy(t, h).start()
+
+        g_copy(t, other).start()
+        return 0
+
+    lax.fori_loop(0, nc, start_g, 0)
+    g_all[h, c] = g_s[...]
+
+    def col_copy(zz, core):
+        return remote(p_z.at[zz], pc_all.at[h, c], send_pc.at[core, zz], recv_pc.at[h, c], at(z, core, zz))
+
+    def pass_pz(t, _):
+        zz = lax.rem(z + near_first(t - 1, nz), nz)
+
+        @pl.when(t > 0)
+        def _():
+            line_arrival(p_z, 9, zz).wait_recv()
+
+        @pl.when(zz == c)
+        def _():
+            pc_all[h, c] = p_z[zz]
+
+        @pl.when(zz != c)
+        def _():
+            col_copy(zz, h).start()
+
+        col_copy(zz, other).start()
+        return 0
+
+    lax.fori_loop(0, nz, pass_pz, 0)
+
+    def wait_pred(t, _):
+        line_arrival(pz_r, 8, lax.rem(z + t, nz)).wait_recv()
+        return 0
+
+    lax.fori_loop(1, nz, wait_pred, 0)
     pred_s[...] = jnp.sum(pz_r[...], axis=0)
     swap_pred = remote(pred_s, pred_r, pair_s.at[4], pair_r.at[4], at(z, other, c))
     swap_pred.start()
-
-    def g_copy(t, core):
-        return remote(g_s, g_all.at[h, c], send_g.at[core, t], recv_g.at[h, c], at(z, core, lax.rem(c + t, nc)))
-
-    def g_arrival(core, p):
-        return remote(g_s, g_all.at[core, p], send_g.at[0, 0], recv_g.at[core, p], at(z, other, c))
-
-    def start_g(t, _):
-        @pl.when(t > 0)
-        def _():
-            g_copy(t, h).start()
-
-        g_copy(t, other).start()
-        return 0
-
-    lax.fori_loop(0, nc, start_g, 0)
-    g_all[h, c] = g_s[...]
-
-    def col_copy(zz, core):
-        return remote(p_z.at[zz], pc_all.at[h, c], send_pc.at[core, zz], recv_pc.at[h, c], at(z, core, zz))
-
-    def pass_pz(t, _):
-        zz = lax.rem(z + near_first(t - 1, nz), nz)
-
-        @pl.when(t > 0)
-        def _():
-            line_arrival(p_z, 9, zz).wait_recv()
-
-        @pl.when(zz == c)
-        def _():
-            pc_all[h, c] = p_z[zz]
-
-        @pl.when(zz != c)
-        def _():
-            col_copy(zz, h).start()
-
-        col_copy(zz, other).start()
-        return 0
-
-    lax.fori_loop(0, nz, pass_pz, 0)
 
     def wait_g(t, _):
         p = lax.rem(c + t, nc)
@@ -528,19 +561,7 @@
     coeffs = jnp.dot(jnp.broadcast_to(diff, (8, tokens)), inv, precision=HI, preferred_element_type=jnp.float32)
     shift_out[...] = jnp.dot(coeffs, pr, precision=HI, preferred_element_type=jnp.float32)[:1]
 
-    for block in range(4):
-        swap_x(block).wait_send()
-
     def sent(t, _):
-        ctx_copy(t).wait_send()
-        remote(phi_s, z_recv.at[z], send.at[1, t], recv.at[1, z], at(lax.rem(z + t, nz), h, c)).wait_send()
-        line_copy(phi_s, phi_c.at[h * nz + z], 2, t).wait_send()
-
-        @pl.when(lax.rem(c + t, nc) != z)
-        def _():
-            pass_row(t).wait_send()
-
-        plane_copy(pp_send.at[lax.rem(c + t, nc)], pp_recv.at[c], 5, t).wait_send()
         plane_copy(p_code.at[0], pr_all.at[c], 6, t).wait_send()
         line_copy(gz_s, gz_r.at[z], 7, t).wait_send()
         line_copy(pz_s, pz_r.at[z], 8, t).wait_send()
@@ -551,17 +572,12 @@
     lax.fori_loop(1, nz, sent, 0)
 
     def sent_some(t, _):
-        mate_copy(t).wait_send()
         col_copy(t, other).wait_send()
         g_copy(t, other).wait_send()
 
         @pl.when(t != c)
         def _():
             col_copy(t, h).wait_send()
-
-        @pl.when(jnp.logical_and(holder, t != z))
-        def _():
-            remote(phi_r.at[t], phi_r.at[t], send.at[3, t], recv.at[4, t], at(z, h, t)).wait_send()
 
         return 0
 

time: 77.6 us -> 77 us (level)
  no operation moved by 1% of the time
where the time goes in v8:
time: 77 us; the launch traced here: 76.8 us
  Pallas kernels  76.1 us (99%)
    pallas_call x1, Pallas kernels, exchange(): pl.pallas_call(exchange_kernel, in_specs=[pl.BlockSpec(memory_space=pltpu...  73 us
    pallas_call x1, Pallas kernels, update(): pl.pallas_call(update_kernel, grid=(steps,), in_specs=[whole(*gain.shape)...  3.12 us

profile of v8, /device:TPU:1, one launch (start us, length us, event | category | flops | bytes accessed | tf_op | source)
XLA Modules:
  0.0 76.8 jit_solution(10240178681555067473)
XLA Ops:
  0.6 0.0 copy-start
  0.6 73.0 %shard_map.77 = (bf16[512,384]{1,0:T(8,128)(2,1)S(1)}, bf16[384,1024]{1,0:T(8,128)(2,1)S(1)}, f32[1,512]{1,0:T(1,128)S(1)}) custom-call(bf16[8,256]{1,0:T(8,128)(2,1)} %ctx_hbm.1, bf16[256,1024]{1,0:T(8,128)(2,1)} %w_hbm.1, f32[1,1024]{1,0:T(1,128)} %bitcast.6, f32[512,1024]{1,0:T(8,128)} %cov_ref.1, f32[1,512]{1,0:T(1,128)} %bitcast.4, f32[1,128]{1,0:T(1,128)} %bitcast.7), custom_call_target="tpu_custom_call" | custom-call | tf_op jit(solution)/shard_map/pallas_call | solution.py:607
  73.7 0.0 copy-done
  73.7 3.1 %shard_map.78 = (f32[512,1024]{1,0:T(8,128)}, f32[1,512]{1,0:T(1,128)}) custom-call(bf16[512,384]{1,0:T(8,128)(2,1)S(1)} %get-tuple-element.7.gain_ref, bf16[384,1024]{1,0:T(8,128)(2,1)S(1)} %get-tuple-element.8.pc_ref, f32[1,512]{1,0:T(1,128)S(1)} %get-tuple-element.9.shift_ref, f32[1,512]{1,0:T(1,128)S(1)} %bitcast.5, f32[512,1024]{1,0:T(8,128)} %cov_ref.1), custom_call_target="tpu_custom_call" | custom-call | tf_op jit(solution)/shard_map/pallas_call | solution.py:133
Async XLA Ops:
  0.6 73.0 %copy-start = (f32[512]{0:T(512)S(1)}, f32[512]{0:T(512)}, u32[]{:S(2)}) copy-start(f32[512]{0:T(512)} %param.10) | copy-start | bytes 6148

commit v9 on v8

--- a/solution.py
+++ b/solution.py
@@ -466,6 +466,17 @@
     lax.fori_loop(0, nc, start_g, 0)
     g_all[h, c] = g_s[...]
 
+    def wait_last(t, _):
+        p = lax.rem(c + t, nc)
+        plane_arrival(pr_all, 6, p).wait_recv()
+        return 0
+
+    lax.fori_loop(1, nc, wait_last, 0)
+
+    pr = panel_from(pr_all[...]).reshape(tokens, width)
+    rh, rm, _ = split3(pr.T)
+    pr_t = jnp.concatenate([rh, rh, rm], 1)
+
     def col_copy(zz, core):
         return remote(p_z.at[zz], pc_all.at[h, c], send_pc.at[core, zz], recv_pc.at[h, c], at(z, core, zz))
 
@@ -517,13 +528,6 @@
 
     for lo in range(32, 96, 16):
         blocks = eliminated(blocks, lo, 16)
-
-    def wait_last(t, _):
-        p = lax.rem(c + t, nc)
-        plane_arrival(pr_all, 6, p).wait_recv()
-        return 0
-
-    lax.fori_loop(1, nc, wait_last, 0)
 
     def wait_pc(t, _):
         p = lax.rem(c + t, nc)
@@ -545,9 +549,6 @@
         pc_out[:tokens, cut] = hi
         pc_out[tokens : 2 * tokens, cut] = mid
         pc_out[2 * tokens :, cut] = hi
-    pr = panel_from(pr_all[...]).reshape(tokens, width)
-    rh, rm, _ = split3(pr.T)
-    pr_t = jnp.concatenate([rh, rh, rm], 1)
     for lo in range(96, 128, 16):
         blocks = eliminated(blocks, lo, 16)
     inv = jnp.concatenate(blocks, 0)

time: 77 us -> 76.8 us (level)
  no operation moved by 1% of the time
where the time goes in v9:
time: 76.8 us; the launch traced here: 76.6 us
  Pallas kernels  76 us (99%)
    pallas_call x1, Pallas kernels, exchange(): pl.pallas_call(exchange_kernel, in_specs=[pl.BlockSpec(memory_space=pltpu...  72.9 us
    pallas_call x1, Pallas kernels, update(): pl.pallas_call(update_kernel, grid=(steps,), in_specs=[whole(*gain.shape)...  3.12 us

profile of v9, /device:TPU:1, one launch (start us, length us, event | category | flops | bytes accessed | tf_op | source)
XLA Modules:
  0.0 76.6 jit_solution(12548058076108842496)
XLA Ops:
  0.6 0.0 copy-start
  0.6 72.9 %shard_map.77 = (bf16[512,384]{1,0:T(8,128)(2,1)S(1)}, bf16[384,1024]{1,0:T(8,128)(2,1)S(1)}, f32[1,512]{1,0:T(1,128)S(1)}) custom-call(bf16[8,256]{1,0:T(8,128)(2,1)} %ctx_hbm.1, bf16[256,1024]{1,0:T(8,128)(2,1)} %w_hbm.1, f32[1,1024]{1,0:T(1,128)} %bitcast.6, f32[512,1024]{1,0:T(8,128)} %cov_ref.1, f32[1,512]{1,0:T(1,128)} %bitcast.4, f32[1,128]{1,0:T(1,128)} %bitcast.7), custom_call_target="tpu_custom_call" | custom-call | tf_op jit(solution)/shard_map/pallas_call | solution.py:608
  73.5 0.0 copy-done
  73.5 3.1 %shard_map.78 = (f32[512,1024]{1,0:T(8,128)}, f32[1,512]{1,0:T(1,128)}) custom-call(bf16[512,384]{1,0:T(8,128)(2,1)S(1)} %get-tuple-element.7.gain_ref, bf16[384,1024]{1,0:T(8,128)(2,1)S(1)} %get-tuple-element.8.pc_ref, f32[1,512]{1,0:T(1,128)S(1)} %get-tuple-element.9.shift_ref, f32[1,512]{1,0:T(1,128)S(1)} %bitcast.5, f32[512,1024]{1,0:T(8,128)} %cov_ref.1), custom_call_target="tpu_custom_call" | custom-call | tf_op jit(solution)/shard_map/pallas_call | solution.py:133
Async XLA Ops:
  0.6 72.9 %copy-start = (f32[512]{0:T(512)S(1)}, f32[512]{0:T(512)}, u32[]{:S(2)}) copy-start(f32[512]{0:T(512)} %param.10) | copy-start | bytes 6148
